TPU v7x, 256 devices: a whole 4x4x8 slice. The times are simulated.
256 devices in a mesh: slab: 32 (over z_hi, x, y), chan: 8 (over z_lo, core).
Axes of the slice: x: 4, y: 4, z: 8 (z_hi: 2, z_lo: 4; z = z_hi * 4 + z_lo), core: 2. Of those that a mesh axis runs over, the one named last changes fastest.
Arguments:
- features: bfloat16 [96, 65536], P('chan', 'slab'), may hold values from -1 to 3
- coords: bfloat16 [3, 65536], P(None, 'slab'), may hold values from 0 to 1
- send_rows: int32 [2, 32768], P(None, 'slab'), may hold values from 0 to 2047
- send_count: int32 [2, 32], P(None, 'slab'), may hold values from 1 to 1024, as said below
- neighbours: int32 [4096, 128], P('slab'), may hold values from 0 to 4095, as said below
- neighbour_count: int32 [4096], P('slab'), may hold values from 32 to 128
- geom_weight: bfloat16 [80, 6], replicated, may hold values from -3.5 to 3.5
- feat_weight: bfloat16 [80, 96], replicated, may hold values from -0.625 to 0.625
- bias_one: float32 [80], replicated, may hold values from -3 to 3
- hidden_weight: bfloat16 [80, 80], replicated, may hold values from -1 to 1
- bias_two: float32 [80], replicated, may hold values from -3 to 3
- out_weight: bfloat16 [96, 80], replicated, may hold values from -1 to 1
- bias_three: float32 [96], replicated, may hold values from -3 to 3
Outputs:
- latent: float32 [96, 4096], P('chan', 'slab')
Inputs may be any that keep to these rules, and one draw needn't show every extreme that they name: `send_count`: every slab has at least one live slot in each direction; some slab has all 1024 slots of its lower list live. `neighbours`: entries index the slab's point table: below 2048 own points, then 1024 slots from the slab below, then 1024 from the slab above; slot 0 of every node is an own point; nodes of the lower plane of a slab use the slots from below, those of the upper plane the slots from above, and may name dead slots.
All inputs are finite; a program needn't handle non-finite values.
Results may differ from a plain program's by a relative error of at most 0.0013.
Values may be sent and summed in bfloat16 or wider, within the bound.
A program may use at most 64 MiB of HBM per device.

v0:
```python
import jax
import jax.numpy as jnp
from jax import lax
from jax.sharding import PartitionSpec as P

ZD = 2
GX = 16
GY = 4


def copy_for_each(array, axis):
    length = lax.axis_size(axis)
    return lax.all_to_all(
        jnp.broadcast_to(array[None], (length, *array.shape)), axis, 0, 0, tiled=True
    )


def in_order(parts, dim):
    parts = jnp.moveaxis(parts, 0, dim)
    dims = parts.shape
    return parts.reshape(*dims[:dim], dims[dim] * dims[dim + 1], *dims[dim + 2 :])


def collect(array, axis, dim):
    parts = copy_for_each(array, axis)
    return in_order(parts, dim)


def padded(block, sides, width):
    for axis, dim in sides:
        count = lax.axis_size(axis)
        forward = [(i, i + 1) for i in range(count - 1)]
        backward = [(target, source) for source, target in forward]
        low = lax.ppermute(
            lax.slice_in_dim(block, block.shape[dim] - width, None, axis=dim), axis, forward
        )
        high = lax.ppermute(lax.slice_in_dim(block, 0, width, axis=dim), axis, backward)
        block = jnp.concatenate([low, block, high], axis=dim)
    return block


def node_term(geom_weight, bias_one, node_ids, depth):
    along_x = ((node_ids % GX).astype(jnp.float32) + 0.5) / GX
    along_y = ((node_ids // GX % GY).astype(jnp.float32) + 0.5) / GY
    along_z = ((node_ids // (GX * GY)).astype(jnp.float32) + 0.5) / depth
    geom = geom_weight[:, 0:3].astype(jnp.float32)
    return (
        geom[:, 0:1] * along_x[None, :]
        + geom[:, 1:2] * along_y[None, :]
        + geom[:, 2:3] * along_z[None, :]
        + bias_one[:, None]
    )


def kernel_block(
    pre_table,
    value_table,
    flag_table,
    nbr,
    counts,
    node_pre,
    hidden_weight,
    bias_two,
    out_rows,
    bias_rows,
):
    nodes, slots = nbr.shape
    hidden = pre_table.shape[0]
    flat = nbr.reshape(-1)
    gathered = jnp.take(pre_table, flat, axis=1).astype(jnp.float32).reshape(hidden, nodes, slots)
    first = (
        jax.nn.gelu(gathered + node_pre[:, :, None])
        .reshape(hidden, nodes * slots)
        .astype(jnp.bfloat16)
    )
    second = jax.nn.gelu(
        jnp.dot(hidden_weight, first, preferred_element_type=jnp.float32) + bias_two[:, None]
    ).astype(jnp.bfloat16)
    kappa = jnp.dot(out_rows, second, preferred_element_type=jnp.float32) + bias_rows[:, None]
    values = jnp.take(value_table, flat, axis=1).astype(jnp.float32)
    used = (jnp.arange(slots, dtype=jnp.int32)[None, :] < counts[:, None]).astype(jnp.float32)
    flags = jnp.take(flag_table, flat).astype(jnp.float32) * used.reshape(-1)
    total = (kappa * values * flags[None, :]).reshape(out_rows.shape[0], nodes, slots).sum(axis=2)
    weight = flags.reshape(nodes, slots).sum(axis=1)
    return total / weight[None, :]


def encode(
    pre_table,
    value_table,
    flag_table,
    nbr,
    counts,
    first_id,
    depth,
    geom_weight,
    bias_one,
    hidden_weight,
    bias_two,
    out_rows,
    bias_rows,
):
    nodes = nbr.shape[0]
    block = min(128, nodes)
    blocks = nodes // block

    def one_block(index):
        start = index * block
        ids = first_id + start + jnp.arange(block, dtype=jnp.int32)
        node_pre = node_term(geom_weight, bias_one, ids, depth)
        return kernel_block(
            pre_table,
            value_table,
            flag_table,
            nbr,
            counts,
            node_pre,
            hidden_weight,
            bias_two,
            out_rows,
            bias_rows,
        )

    result = lax.map(one_block, jnp.arange(blocks, dtype=jnp.int32))
    return result.transpose(1, 0, 2).reshape(out_rows.shape[0], nodes)


def shards(
    features,
    coords,
    send_rows,
    send_count,
    neighbours,
    neighbour_count,
    geom_weight,
    feat_weight,
    bias_one,
    hidden_weight,
    bias_two,
    out_weight,
    bias_three,
):
    groups = lax.axis_size("chan")
    member = lax.axis_index("chan")
    slab_id = lax.axis_index("slab")
    depth = ZD * lax.axis_size("slab")
    own_full = collect(features, "chan", 0)
    pre_own = (
        jnp.dot(feat_weight, own_full, preferred_element_type=jnp.float32)
        + jnp.dot(geom_weight[:, 3:6], coords, preferred_element_type=jnp.float32)
    ).astype(jnp.bfloat16)
    send = send_rows.shape[1]
    points = features.shape[1]
    hidden = pre_own.shape[0]
    chans = own_full.shape[0]
    columns = send_rows.reshape(-1)
    live = (
        (jnp.arange(send, dtype=jnp.int32)[None, :] < send_count)
        .astype(jnp.bfloat16)
        .reshape(1, 2 * send)
    )
    pre_sel = jnp.take(pre_own, columns, axis=1)
    val_sel = jnp.take(own_full, columns, axis=1)
    ones_row = jnp.ones((1, 2 * send), jnp.bfloat16)
    payload = jnp.concatenate([pre_sel, val_sel, ones_row], axis=0) * live
    extended = padded(payload, (("slab", 1),), send)
    below = extended[:, :send]
    above = extended[:, 3 * send :]
    below_pre = below[:hidden]
    above_pre = above[:hidden]
    below_vals = below[hidden : hidden + chans]
    above_vals = above[hidden : hidden + chans]
    below_flag = below[hidden + chans]
    above_flag = above[hidden + chans]
    pre_table = jnp.concatenate([pre_own, below_pre, above_pre], axis=1)
    value_table = jnp.concatenate([own_full, below_vals, above_vals], axis=1)
    flag_table = jnp.concatenate(
        [jnp.ones((points,), jnp.bfloat16), below_flag, above_flag], axis=0
    )
    per_slab = neighbours.shape[0]
    share = per_slab // groups
    start = member * share
    part_nbr = lax.dynamic_slice_in_dim(neighbours, start, share, 0)
    part_cnt = lax.dynamic_slice_in_dim(neighbour_count, start, share, 0)
    partial_value = encode(
        pre_table,
        value_table,
        flag_table,
        part_nbr,
        part_cnt,
        slab_id * per_slab + start,
        depth,
        geom_weight,
        bias_one,
        hidden_weight,
        bias_two,
        out_weight,
        bias_three,
    )
    return lax.all_to_all(partial_value, "chan", split_axis=0, concat_axis=1, tiled=True)


def solution(mesh):
    placed = (
        P("chan", "slab"),
        P(None, "slab"),
        P(None, "slab"),
        P(None, "slab"),
        P("slab", None),
        P("slab"),
        P(),
        P(),
        P(),
        P(),
        P(),
        P(),
        P(),
    )
    return jax.shard_map(
        shards, mesh=mesh, in_specs=placed, out_specs=P("chan", "slab"), check_vma=False
    )
```

profile of v0, /device:TPU:31, one launch (start us, length us, event | category | flops | bytes accessed | tf_op | source)
XLA Modules:
  0.0 112.2 jit_solution(15677503354972202036)
XLA Ops:
  0.0 1.7 %broadcast_in_dim.90 = bf16[8,12,2048]{2,1,0:T(8,128)(2,1)} broadcast(bf16[12,2048]{1,0:T(8,128)(2,1)} %param.13), dimensions={1,2} | broadcast | bytes 442368 | tf_op jit(solution)/shard_map/broadcast_in_dim | solution.py:14
  1.7 6.6 %all-to-all-start = ((bf16[8,12,2048]{2,1,0:T(8,128)(2,1)}), bf16[8,12,2048]{2,1,0:T(8,128)(2,1)S(1)}, u32[]{:S(2)}, u32[]{:S(2)}) async-start(bf16[8,12,2048]{2,1,0:T(8,128)(2,1)} %broadcast_in_dim.90), calls=%async_computation | async-start | bytes 1048576 | tf_op jit(solution)/shard_map/all_to_all | solution.py:13
  8.4 0.1 fusion.39
  8.5 0.7 constant_dynamic-slice_fusion
  9.2 0.1 pad.11.clone
  9.3 13.3 %all-to-all-done = bf16[8,12,2048]{2,1,0:T(8,128)(2,1)S(1)} async-done(((bf16[8,12,2048]{2,1,0:T(8,128)(2,1)}), bf16[8,12,2048]{2,1,0:T(8,128)(2,1)S(1)}, u32[]{:S(2)}, u32[]{:S(2)}) %all-to-all-start) | async-done | bytes 393248 | tf_op jit(solution)/shard_map/all_to_all | solution.py:13
  22.7 0.1 reshape.340
  22.8 0.3 copy.59
  23.1 0.2 fusion.61
  23.3 0.2 copy-done.4
  23.5 0.3 fusion.3
  23.8 0.3 copy.57
  24.1 6.2 %gather_fusion = bf16[2048,80]{1,0:T(8,128)(2,1)S(1)} fusion(bf16[80,2048]{0,1:T(8,128)(2,1)S(1)} %copy.57, s32[2048]{0:T(1024)S(1)} %broadcast_clamp_fusion.1), kind=kCustom, calls=%fused_computation | custom fusion | bytes 663552 | tf_op jit(solution)/shard_map/jit(_take)/gather | solution.py:162
  30.2 0.2 copy.58
  30.5 6.2 %gather_fusion.1 = bf16[2048,96]{1,0:T(8,128)(2,1)S(1)} fusion(bf16[96,2048]{0,1:T(8,128)(2,1)S(1)} %copy.59, s32[2048]{0:T(1024)S(1)} %broadcast_clamp_fusion.1), kind=kCustom, calls=%fused_computation.1 | custom fusion | bytes 794624 | tf_op jit(solution)/shard_map/jit(_take)/gather | solution.py:163
  36.7 0.2 copy.60
  37.0 0.2 maximum_multiply_fusion
  37.3 5.9 %collective-permute-start = (bf16[177,1024]{1,0:T(8,128)(2,1)S(1)}, bf16[177,1024]{1,0:T(8,128)(2,1)S(1)}, u32[]{:S(2)}, u32[]{:S(2)}) collective-permute-start(bf16[177,1024]{1,0:T(8,128)(2,1)S(1)} %get-tuple-element.33), channel_id=1, source_target_pairs={{0,8},{8,16},{16,24},{24,32},{32,40},{40,48},{48,56},{56,64},{64,7... | collective-permute-start | bytes 1087496 | tf_op jit(solution)/shard_map/ppermute | solution.py:34
  43.2 1.9 %collective-permute-start.1 = (bf16[177,1024]{1,0:T(8,128)(2,1)S(1)}, bf16[177,1024]{1,0:T(8,128)(2,1)S(1)}, u32[]{:S(2)}, u32[]{:S(2)}) collective-permute-start(bf16[177,1024]{1,0:T(8,128)(2,1)S(1)} %get-tuple-element.34), channel_id=1, source_target_pairs={{8,0},{16,8},{24,16},{32,24},{40,32},{48,40},{56,48},{64,56},{72,6... | collective-permute-start | bytes 1087496 | tf_op jit(solution)/shard_map/ppermute | solution.py:37
  45.2 0.1 add_add_fusion
  45.3 0.1 copy.63
  45.4 4.9 %collective-permute-done = bf16[177,1024]{1,0:T(8,128)(2,1)S(1)} collective-permute-done((bf16[177,1024]{1,0:T(8,128)(2,1)S(1)}, bf16[177,1024]{1,0:T(8,128)(2,1)S(1)}, u32[]{:S(2)}, u32[]{:S(2)}) %collective-permute-start) | collective-permute-done | bytes 362528 | tf_op jit(solution)/shard_map/ppermute | solution.py:34
  50.4 11.9 %collective-permute-done.1 = bf16[177,1024]{1,0:T(8,128)(2,1)S(1)} collective-permute-done((bf16[177,1024]{1,0:T(8,128)(2,1)S(1)}, bf16[177,1024]{1,0:T(8,128)(2,1)S(1)}, u32[]{:S(2)}, u32[]{:S(2)}) %collective-permute-start.1) | collective-permute-done | bytes 362528 | tf_op jit(solution)/shard_map/ppermute | solution.py:37
  62.4 13.1 %gather_fusion.4 = bf16[2048]{0:T(1024)(128)(2,1)S(1)} fusion(bf16[4096]{0:T(1024)(128)(2,1)S(1)} %pad_maximum_fusion.2, s32[2048]{0:T(1024)S(1)} %broadcast_clamp_fusion), kind=kCustom, calls=%fused_computation.4 | custom fusion | bytes 16384 | tf_op jit(solution)/shard_map/while/body/eval_jaxpr/jit(_take)/gather | solution.py:82
  75.5 0.9 select_reduce_fusion
  76.4 0.8 convert_select_fusion
  77.1 0.2 copy.65
  77.3 0.2 copy.66
  77.5 0.2 pad_maximum_fusion
  77.7 6.2 %gather_fusion.3 = bf16[2048,96]{1,0:T(8,128)(2,1)S(1)} fusion(bf16[96,4096]{0,1:T(8,128)(2,1)S(1)} %pad_maximum_fusion, s32[2048]{0:T(1024)S(1)} %broadcast_clamp_fusion), kind=kCustom, calls=%fused_computation.3 | custom fusion | bytes 794624 | tf_op jit(solution)/shard_map/while/body/eval_jaxpr/jit(_take)/gather | solution.py:80
  83.9 0.2 copy.67
  84.2 0.9 slice.78
  85.2 0.7 copy.61
  85.9 6.2 %gather_fusion.2 = bf16[2048,80]{1,0:T(8,128)(2,1)S(1)} fusion(bf16[80,4096]{0,1:T(8,128)(2,1)S(1)} %copy.61, s32[2048]{0:T(1024)S(1)} %broadcast_clamp_fusion), kind=kCustom, calls=%fused_computation.2 | custom fusion | bytes 663552 | tf_op jit(solution)/shard_map/while/body/eval_jaxpr/jit(_take)/gather | solution.py:70
  92.1 0.2 copy.62
  92.3 0.2 add.268
  92.6 0.2 copy-done.8
  92.8 0.8 fusion.4
  93.6 0.1 copy.76
  93.8 0.3 reduce_sum.22
  94.1 0.1 reduce_sum.23
  94.2 0.1 broadcast_divide_fusion
  94.3 0.1 reshape.389
  94.4 15.8 %all_to_all.21 = f32[8,1,192]{2,1,0:T(1,128)S(1)} all-to-all(f32[8,1,192]{2,1,0:T(1,128)S(1)} %reshape.389), channel_id=1, replica_groups=mesh['slab'=32,'chan'=8] {'chan'}, dimensions={0} | all-to-all | bytes 12288 | tf_op jit(solution)/shard_map/all_to_all | solution.py:200
  110.2 0.5 broadcast.490
  110.8 0.7 reduce.4
  111.4 0.1 reshape.390
  111.5 0.7 copy.71
  (47 shorter events, 0.6 us)
Async XLA Ops:
  0.0 92.6 %copy-start = (bf16[96,80]{0,1:T(8,128)(2,1)S(1)}, bf16[96,80]{0,1:T(8,128)(2,1)}, u32[]{:S(2)}) copy-start(bf16[96,80]{0,1:T(8,128)(2,1)} %param.24) | copy-start | bytes 46084
  0.0 8.3 %copy-start.2 = (s32[2,1024]{1,0:T(2,128)S(1)}, s32[2,1024]{1,0:T(2,128)}, u32[]{:S(2)}) copy-start(s32[2,1024]{1,0:T(2,128)} %param.15) | copy-start | bytes 24580
  0.0 8.3 %copy-start.5 = (bf16[80,6]{0,1:T(8,128)(2,1)S(1)}, bf16[80,6]{0,1:T(8,128)(2,1)}, u32[]{:S(2)}) copy-start(bf16[80,6]{0,1:T(8,128)(2,1)} %param.19) | copy-start | bytes 2884
  0.0 8.4 %copy-start.6 = (s32[2,1]{0,1:T(1,128)S(1)}, s32[2,1]{0,1:T(1,128)}, u32[]{:S(2)}) copy-start(s32[2,1]{0,1:T(1,128)} %param.16) | copy-start | bytes 28
  1.7 20.9 %all-to-all-start = ((bf16[8,12,2048]{2,1,0:T(8,128)(2,1)}), bf16[8,12,2048]{2,1,0:T(8,128)(2,1)S(1)}, u32[]{:S(2)}, u32[]{:S(2)}) async-start(bf16[8,12,2048]{2,1,0:T(8,128)(2,1)} %broadcast_in_dim.90), calls=%async_computation | async-start | bytes 1048576 | tf_op jit(solution)/shard_map/all_to_all | solution.py:13
  8.3 14.7 %copy-start.3 = (bf16[80,96]{1,0:T(8,128)(2,1)S(1)}, bf16[80,96]{1,0:T(8,128)(2,1)}, u32[]{:S(2)}) copy-start(bf16[80,96]{1,0:T(8,128)(2,1)} %param.20) | copy-start | bytes 46084
  22.8 0.7 copy-start.4
  37.2 7.9 %copy-start.7 = (f32[80]{0:T(128)S(1)}, f32[80]{0:T(128)}, u32[]{:S(2)}) copy-start(f32[80]{0:T(128)} %param.21) | copy-start | bytes 964
  37.2 8.0 %copy-start.9 = (s32[128]{0:T(128)S(1)}, s32[128]{0:T(128)}, u32[]{:S(2)}) copy-start(s32[128]{0:T(128)} %param.18) | copy-start | bytes 1540
  37.3 13.1 %collective-permute-start = (bf16[177,1024]{1,0:T(8,128)(2,1)S(1)}, bf16[177,1024]{1,0:T(8,128)(2,1)S(1)}, u32[]{:S(2)}, u32[]{:S(2)}) collective-permute-start(bf16[177,1024]{1,0:T(8,128)(2,1)S(1)} %get-tuple-element.33), channel_id=1, source_target_pairs={{0,8},{8,16},{16,24},{24,32},{32,40},{40,48},{48,56},{56,64},{64,7... | collective-permute-start | bytes 1087496 | tf_op jit(solution)/shard_map/ppermute | solution.py:34
  43.2 19.1 %collective-permute-start.1 = (bf16[177,1024]{1,0:T(8,128)(2,1)S(1)}, bf16[177,1024]{1,0:T(8,128)(2,1)S(1)}, u32[]{:S(2)}, u32[]{:S(2)}) collective-permute-start(bf16[177,1024]{1,0:T(8,128)(2,1)S(1)} %get-tuple-element.34), channel_id=1, source_target_pairs={{8,0},{16,8},{24,16},{32,24},{40,32},{48,40},{56,48},{64,56},{72,6... | collective-permute-start | bytes 1087496 | tf_op jit(solution)/shard_map/ppermute | solution.py:37
  62.3 15.0 %copy-start.1 = (bf16[177,1024]{1,0:T(8,128)(2,1)}, bf16[177,1024]{1,0:T(8,128)(2,1)S(1)}, u32[]{:S(2)}) copy-start(bf16[177,1024]{1,0:T(8,128)(2,1)S(1)} %collective-permute-done.1) | copy-start | bytes 1087492
  92.1 0.7 copy-start.8
  92.1 0.7 copy-start.10
  92.1 0.7 copy-start.11
where the time goes:
time: 113 us; the launch traced here: 112 us
  local copies, waits for them, and re-layouts  46.5 us (41%)
  waiting for transfers between devices  30.2 us (27%)
  blocking collectives  15.8 us (14%)
  starting transfers between devices  14.4 us (13%)
  other arithmetic  3.49 us (3%)
  matrix products  1.32 us (1%)
    all_to_all x1, blocking collectives, shards(): lax.all_to_all(partial_value, 'chan', split_axis=0, concat_axis=1, tiled=...  15.8 us
    all_to_all x1, waiting for transfers between devices, copy_for_each(): lax.all_to_all(jnp.broadcast_to(array[None], (length, *array.shape)), axi...  13.3 us
    gather x1, local copies, waits for them, and re-layouts, kernel_block(): flags = jnp.take(flag_table, flat).astype(jnp.float32) * used.reshape(-1)  13.1 us
    ppermute x1, waiting for transfers between devices, padded(): lax.ppermute(lax.slice_in_dim(block, 0, width, axis=dim), axis, backward)  11.9 us
    all_to_all x1, starting transfers between devices, copy_for_each(): lax.all_to_all(jnp.broadcast_to(array[None], (length, *array.shape)), axi...  6.57 us
    gather x2, local copies, waits for them, and re-layouts, shards(): val_sel = jnp.take(own_full, columns, axis=1)  6.4 us
    gather x2, local copies, waits for them, and re-layouts, kernel_block(): values = jnp.take(value_table, flat, axis=1).astype(jnp.float32)  6.4 us
    gather x2, local copies, waits for them, and re-layouts, shards(): pre_sel = jnp.take(pre_own, columns, axis=1)  6.39 us
  transfers between devices with their start and end apart: 3, of which 3 were waited for; matrix products, arithmetic and copies ran while one was open for 1% of the time, Pallas kernels for 0%

commit v1 on v0

v1 whole, which is shorter than its diff:
```python
import functools

import jax
import jax.numpy as jnp
from jax import lax
from jax.experimental import pallas as pl
from jax.experimental.pallas import tpu as pltpu
from jax.sharding import PartitionSpec as P

MESH = pl.DeviceIdType.MESH
ZD = 2
GX = 16
GY = 4
F32 = jnp.float32
BF16 = jnp.bfloat16
ROWS = 16
BLK = 256
C0 = 0.7978845608028654
C1 = 0.7978845608028654 * 0.044715


def gelu(x):
    half = 0.5 * x
    return half + half * jnp.tanh(x * (C0 + C1 * (x * x)))


def iota(shape, dim):
    return lax.broadcasted_iota(jnp.int32, shape, dim)


def one_hot(index, ramp):
    row = jnp.broadcast_to(index, (16, index.shape[1])).astype(BF16)
    full = jnp.concatenate([row] * (BLK // 16), axis=0)
    return jnp.where(ramp == full, jnp.ones_like(full), jnp.zeros_like(full))


def kernel(
    slabs,
    feat,
    coords,
    send_rows,
    send_count,
    nbr,
    counts,
    geom_t,
    feat_weight,
    bias_one,
    hidden_weight,
    bias_two,
    out_t,
    bias_three,
    out,
    own,
    halo,
    picked,
    hot,
    grid,
    stage,
    small,
    wide,
    w_pre,
    w_out,
    res,
    rcv,
    own_send,
    own_recv,
    own_fwd,
    halo_send,
    halo_recv,
    halo_fwd,
    res_send,
    res_recv,
):
    s = lax.axis_index("slab")
    c = lax.axis_index("chan")
    chip = c // 2
    core = c % 2
    sib = c + 1 - 2 * core
    upper = c // 4
    has_up = s < slabs - 1
    has_down = s > 0
    has_halo = jnp.where(upper == 1, s < slabs - 1, s > 0)
    source_slab = s - 1 + 2 * upper
    points = feat.shape[1]
    send = send_rows.shape[1]

    barrier = pltpu.get_barrier_semaphore()
    for j in range(1, 8):
        pl.semaphore_signal(barrier, inc=1, device_id=(s, (c + j) % 8), device_id_type=MESH)

    @pl.when(has_halo)
    def _():
        for q in range(4):
            pl.semaphore_signal(
                barrier, inc=1, device_id=(source_slab, 2 * q + core), device_id_type=MESH
            )

    stage[0:12, :] = feat[...].astype(F32)
    stage[12:15, :] = coords[...].astype(F32)
    stage[15:16, :] = jnp.ones((1, points), F32)
    slot = stage[...].astype(BF16)
    own[c] = slot

    ramp = iota((BLK, 128), 0).astype(F32).astype(BF16)
    pieces = points // BLK
    stacked = jnp.concatenate([slot[:, h * BLK : (h + 1) * BLK] for h in range(pieces)], axis=0)
    for d in range(2):
        for j in range(send // BLK):
            idx = send_rows[d : d + 1, j * BLK : (j + 1) * BLK]
            idx = jnp.where(iota((1, BLK), 1) + j * BLK < send_count[d], idx, -1)
            low = (idx & (BLK - 1)).astype(F32)
            high = lax.shift_right_arithmetic(idx, 8)
            hots = jnp.concatenate(
                [one_hot(low[:, t * 128 : (t + 1) * 128], ramp) for t in range(BLK // 128)], axis=1
            )
            parts = jnp.dot(stacked, hots, preferred_element_type=F32)
            total = jnp.zeros((ROWS, BLK), F32)
            for h in range(pieces):
                total = total + jnp.where(high == h, parts[h * ROWS : (h + 1) * ROWS], 0.0)
            picked[d, :, j * BLK : (j + 1) * BLK] = total.astype(BF16)

    pl.semaphore_wait(barrier, 7 + 2 * jnp.where(has_up, 1, 0) + 2 * jnp.where(has_down, 1, 0))

    def halo_copy(d, q):
        target = (s + 1, 2 * q + core) if d == 1 else (s - 1, 4 + 2 * q + core)
        return pltpu.make_async_remote_copy(
            src_ref=picked.at[d],
            dst_ref=halo.at[c],
            send_sem=halo_send.at[d, q],
            recv_sem=halo_recv.at[c],
            device_id=target,
            device_id_type=MESH,
        )

    def own_copy(j):
        target = sib if j == 0 else 2 * ((chip + j) % 4) + core
        return pltpu.make_async_remote_copy(
            src_ref=own.at[c],
            dst_ref=own.at[c],
            send_sem=own_send.at[j],
            recv_sem=own_recv.at[c],
            device_id=(s, target),
            device_id_type=MESH,
        )

    @pl.when(has_up)
    def _():
        for q in range(2):
            halo_copy(1, q).start()

    @pl.when(has_down)
    def _():
        for q in range(2):
            halo_copy(0, q).start()

    for j in range(4):
        own_copy(j).start()

    small[...] = jnp.zeros_like(small)
    small[0:6, 0:80] = geom_t[...].astype(F32)
    small[6:7, 0:80] = bias_one[...]
    small[7:8, 0:80] = bias_two[...]
    lane = iota((96, 128), 1)
    spread = jnp.where(
        (lane // ROWS * 12 + lane % ROWS == iota((96, 128), 0)) & (lane % ROWS < 12), 1.0, 0.0
    )
    b3 = jnp.dot(
        jnp.broadcast_to(bias_three[...], (8, 96)),
        spread,
        preferred_element_type=F32,
        precision=lax.Precision.HIGHEST,
    )
    small[8:16, :] = jnp.where(iota((8, 128), 1) % ROWS == ROWS - 1, 1.0, b3)
    cols = jnp.transpose(small[...])
    spread = spread.astype(BF16)
    lane80 = iota((80, 128), 1)
    wide_pre = jnp.dot(feat_weight[...], spread, preferred_element_type=F32)
    for i in range(3):
        wide_pre = jnp.where(lane80 == 12 + i, cols[0:80, 3 + i : 4 + i], wide_pre)
    w_pre[...] = wide_pre.astype(BF16)
    small[0:80, :] = jnp.dot(out_t[...], spread, preferred_element_type=F32)
    w_out[...] = jnp.transpose(small[...])[:, 0:80].astype(BF16)
    along_y = ((c % GY).astype(F32) + 0.5) / GY
    along_z = ((2 * s + upper).astype(F32) + 0.5) / (ZD * slabs)
    wide[0:80, :] = jnp.broadcast_to(cols[0:80, 0:1], (80, 128))
    wide[80:160, :] = jnp.broadcast_to(
        cols[0:80, 1:2] * along_y + cols[0:80, 2:3] * along_z + cols[0:80, 6:7], (80, 128)
    )
    wide[160:240, :] = jnp.broadcast_to(cols[0:80, 7:8], (80, 128))
    wide[240:368, :] = jnp.broadcast_to(cols[:, 8:9], (128, 128))

    first = pl.multiple_of(c * 16, 16)
    idx = nbr[pl.ds(first, 16), :]
    idx = idx - jnp.where(idx >= points, send * upper, 0)
    slots = iota((1, 128), 1)
    rows = []
    for n in range(16):
        rows.append(jnp.where(slots < counts[first + n], idx[n : n + 1, :], -1))
    lows = [(r & (BLK - 1)).astype(F32) for r in rows]
    highs = [lax.shift_right_arithmetic(r, 8) for r in rows]

    def build(kb, carry):
        at = pl.ds(pl.multiple_of(kb * BLK, BLK), BLK)
        for n in range(16):
            pick = jnp.where(highs[n] == kb, lows[n], -1.0)
            hot[at, n * 128 : (n + 1) * 128] = one_hot(pick, ramp)
        return carry

    lax.fori_loop(0, (points + send) // BLK, build, 0)

    def landed(buf, sem, i):
        return pltpu.make_async_remote_copy(
            src_ref=buf.at[i],
            dst_ref=buf.at[i],
            send_sem=sem.at[i],
            recv_sem=sem.at[i],
            device_id=(s, sib),
            device_id_type=MESH,
        )

    def forward(buf, fwd, recv, i, k):
        return pltpu.make_async_remote_copy(
            src_ref=buf.at[i],
            dst_ref=buf.at[i],
            send_sem=fwd.at[k],
            recv_sem=recv.at[i],
            device_id=(s, sib),
            device_id_type=MESH,
        )

    for j in range(1, 4):
        i = 2 * ((chip + j) % 4) + core
        landed(own, own_recv, i).wait_recv()
        forward(own, own_fwd, own_recv, i, j - 1).start()
    for j in range(4):
        landed(own, own_recv, 2 * ((chip + j) % 4) + 1 - core).wait_recv()

    table = own[...].reshape(8 * ROWS, points)

    def gather_own(b, carry):
        at = pl.ds(pl.multiple_of(b * BLK, BLK), BLK)
        grid[:, at] = jnp.dot(table, hot[0:points, at], preferred_element_type=F32)
        return carry

    lax.fori_loop(0, 2048 // BLK, gather_own, 0)

    @pl.when(has_halo)
    def _():
        for q in range(4):
            i = 2 * q + core
            landed(halo, halo_recv, i).wait_recv()
            forward(halo, halo_fwd, halo_recv, i, q).start()
        for q in range(4):
            landed(halo, halo_recv, 2 * q + 1 - core).wait_recv()

    @pl.when(jnp.logical_not(has_halo))
    def _():
        halo[...] = jnp.zeros_like(halo)

    side = halo[...].reshape(8 * ROWS, send)
    w1 = w_pre[...]
    w2 = hidden_weight[...]
    w3 = w_out[...]

    def block(b, acc):
        at = pl.ds(pl.multiple_of(b * BLK, BLK), BLK)
        values = grid[:, at] + jnp.dot(
            side, hot[points : points + send, at], preferred_element_type=F32
        )
        pre = jnp.dot(w1, values.astype(BF16), preferred_element_type=F32)
        pre = pre.astype(BF16).astype(F32)
        x0 = ((2 * b).astype(F32) + 0.5) / GX
        x1 = ((2 * b + 1).astype(F32) + 0.5) / GX
        base = wide[80:160, :]
        slope = wide[0:80, :]
        node = jnp.concatenate([base + slope * x0, base + slope * x1], axis=1)
        h1 = gelu(pre + node).astype(BF16)
        b2 = wide[160:240, :]
        h2 = jnp.dot(w2, h1, preferred_element_type=F32) + jnp.concatenate([b2, b2], axis=1)
        h2 = gelu(h2).astype(BF16)
        b3w = wide[240:368, :]
        kappa = jnp.dot(w3, h2, preferred_element_type=F32) + jnp.concatenate([b3w, b3w], axis=1)
        prod = kappa * values
        top = prod.astype(BF16)
        rest = (prod - top.astype(F32)).astype(BF16)
        place = c * 16 + 2 * b + iota((BLK, 128), 0) // 128
        seg = jnp.where(iota((BLK, 128), 1) == place, 1.0, 0.0).astype(BF16)
        return (
            acc
            + jnp.dot(top, seg, preferred_element_type=F32)
            + jnp.dot(rest, seg, preferred_element_type=F32)
        )

    acc = lax.fori_loop(0, 2048 // BLK, block, jnp.zeros((128, 128), F32))
    mine = iota((128, 128), 1) // 16 == c
    number = jnp.where(mine, jnp.broadcast_to(acc[15:16, :], (128, 128)), 1.0)
    res[...] = jnp.where(mine, acc / number, 0.0).reshape(8, ROWS, 128)

    def res_copy(j):
        target = (c + j) % 8
        return pltpu.make_async_remote_copy(
            src_ref=res.at[target],
            dst_ref=rcv.at[c],
            send_sem=res_send.at[j - 1],
            recv_sem=res_recv.at[c],
            device_id=(s, target),
            device_id_type=MESH,
        )

    for j in range(1, 8):
        res_copy(j).start()
    rcv[c] = res[c]

    for j in range(4):
        own_copy(j).wait_send()
    for j in range(1, 4):
        i = 2 * ((chip + j) % 4) + core
        forward(own, own_fwd, own_recv, i, j - 1).wait_send()

    @pl.when(has_up)
    def _():
        for q in range(2):
            halo_copy(1, q).wait_send()

    @pl.when(has_down)
    def _():
        for q in range(2):
            halo_copy(0, q).wait_send()

    @pl.when(has_halo)
    def _():
        for q in range(4):
            forward(halo, halo_fwd, halo_recv, 2 * q + core, q).wait_send()

    for j in range(1, 8):
        landed(rcv, res_recv, (c + j) % 8).wait_recv()
    for j in range(1, 8):
        res_copy(j).wait_send()
    out[...] = rcv[...].sum(axis=0)[0:12, :]


def shards(
    slabs,
    features,
    coords,
    send_rows,
    send_count,
    neighbours,
    neighbour_count,
    geom_weight,
    feat_weight,
    bias_one,
    hidden_weight,
    bias_two,
    out_weight,
    bias_three,
):
    points = features.shape[1]
    send = send_rows.shape[1]
    vmem = pl.BlockSpec(memory_space=pltpu.VMEM)
    smem = pl.BlockSpec(memory_space=pltpu.SMEM)
    dma = pltpu.SemaphoreType.DMA
    return pl.pallas_call(
        functools.partial(kernel, slabs),
        out_shape=jax.ShapeDtypeStruct((12, 128), F32),
        in_specs=[vmem, vmem, vmem, smem, vmem, smem] + [vmem] * 7,
        out_specs=vmem,
        scratch_shapes=[
            pltpu.VMEM((8, ROWS, points), BF16),
            pltpu.VMEM((8, ROWS, send), BF16),
            pltpu.VMEM((2, ROWS, send), BF16),
            pltpu.VMEM((points + send, 2048), BF16),
            pltpu.VMEM((8 * ROWS, 2048), F32),
            pltpu.VMEM((ROWS, points), F32),
            pltpu.VMEM((128, 128), F32),
            pltpu.VMEM((368, 128), F32),
            pltpu.VMEM((80, 128), BF16),
            pltpu.VMEM((128, 80), BF16),
            pltpu.VMEM((8, ROWS, 128), F32),
            pltpu.VMEM((8, ROWS, 128), F32),
            dma((4,)),
            dma((8,)),
            dma((3,)),
            dma((2, 2)),
            dma((8,)),
            dma((4,)),
            dma((7,)),
            dma((8,)),
        ],
        compiler_params=pltpu.CompilerParams(
            collective_id=0, has_side_effects=True, vmem_limit_bytes=60 * 2**20
        ),
    )(
        features,
        coords,
        send_rows,
        send_count.reshape(2),
        neighbours,
        neighbour_count,
        geom_weight.T,
        feat_weight,
        bias_one.reshape(1, -1),
        hidden_weight,
        bias_two.reshape(1, -1),
        out_weight.T,
        bias_three.reshape(1, -1),
    )


def solution(mesh):
    placed = (
        P("chan", "slab"),
        P(None, "slab"),
        P(None, "slab"),
        P(None, "slab"),
        P("slab", None),
        P("slab"),
        P(),
        P(),
        P(),
        P(),
        P(),
        P(),
        P(),
    )
    return jax.shard_map(
        functools.partial(shards, mesh.shape["slab"]),
        mesh=mesh,
        in_specs=placed,
        out_specs=P("chan", "slab"),
        check_vma=False,
    )
```

time: 113 us -> 37.9 us (0.34)
  local copies, waits for them, and re-layouts: 46.5 us -> 1.3 us
  Pallas kernels: 0 us -> 36.4 us
  waiting for transfers between devices: 30.2 us -> 0 us
  blocking collectives: 15.8 us -> 0 us
  starting transfers between devices: 14.4 us -> 0 us
  other arithmetic: 3.49 us -> 0 us
  matrix products: 1.32 us -> 0 us
    gather x9 -> x0, local copies, waits for them, and re-layouts: 38.7 us -> none  [the longest x1 13.1 us: kernel_block(): flags = jnp.take(flag_table, flat).astype(jnp.float32) * used.reshape(-1)]
    pallas_call x0 -> x1, Pallas kernels: none -> 36.4 us  [shards(): pl.pallas_call(functools.partial(kernel, slabs), out_shape=jax.ShapeDtype...]
    ppermute x2 -> x0, waiting for transfers between devices: 16.9 us -> none  [the longest x1 11.9 us: padded(): lax.ppermute(lax.slice_in_dim(block, 0, width, axis=dim), axis, backward)]
    all_to_all x1 -> x0, blocking collectives: 15.8 us -> none  [shards(): lax.all_to_all(partial_value, 'chan', split_axis=0, concat_axis=1, tiled=...]
    all_to_all x1 -> x0, waiting for transfers between devices: 13.3 us -> none  [copy_for_each(): lax.all_to_all(jnp.broadcast_to(array[None], (length, *array.shape)), axi...]
    ppermute x2 -> x0, starting transfers between devices: 7.84 us -> none  [the longest x1 5.92 us: padded(): lax.ppermute(lax.slice_in_dim(block, block.shape[dim] - width, None, axis...]
    all_to_all x1 -> x0, starting transfers between devices: 6.57 us -> none  [copy_for_each(): lax.all_to_all(jnp.broadcast_to(array[None], (length, *array.shape)), axi...]
    broadcast_in_dim x2 -> x0, local copies, waits for them, and re-layouts: 1.72 us -> none  [the longest x1 1.71 us: copy_for_each(): jnp.broadcast_to(array[None], (length, *array.shape))]
  transfers between devices with their start and end apart: 3 -> 0, of which waited for: 3 -> 0; matrix products, arithmetic and copies ran while one was open for 1% -> 0% of each run, Pallas kernels for 0% -> 0%
where the time goes in v1:
time: 37.9 us; the launch traced here: 37.7 us
  Pallas kernels  36.4 us (96%)
  local copies, waits for them, and re-layouts  1.3 us (3%)
    pallas_call x1, Pallas kernels, shards(): pl.pallas_call(functools.partial(kernel, slabs), out_shape=jax.ShapeDtype...  36.4 us
    unnamed x1, local copies, waits for them, and re-layouts  1.3 us

profile of v1, /device:TPU:31, one launch (start us, length us, event | category | flops | bytes accessed | tf_op | source)
XLA Modules:
  0.0 37.7 jit_solution(7819623969246488701)
XLA Ops:
  0.0 36.4 %shard_map.127 = f32[12,128]{1,0:T(8,128)} custom-call(bf16[12,2048]{1,0:T(8,128)(2,1)} %feat.1, bf16[3,2048]{1,0:T(4,128)(2,1)} %coords.1, s32[2,1024]{1,0:T(2,128)} %send_rows.1, s32[2]{0:T(128)} %bitcast.8, s32[128,128]{1,0:T(8,128)} %nbr.1, s32[128]{0:T(128)} %counts.1, bf16[6,80]{1,0:T(8,128)(2,1)} %bitcast.7, bf16[80,96]{1,0:T(8,128)(2,1)} %feat_weight.1, ...), custom_call_target="tpu_custom_call" | custom-call | tf_op jit(solution)/shard_map/pallas_call | solution.py:363
  36.4 1.3 %copy.15 = f32[12,128]{1,0:T(8,128)} copy(f32[12,128]{1,0:T(8,128)} %shard_map.127) | data formatting | bytes 12288

commit v2 on v1

v2 whole, which is shorter than its diff:
```python
import functools

import jax
import jax.numpy as jnp
from jax import lax
from jax.experimental import pallas as pl
from jax.experimental.pallas import tpu as pltpu
from jax.sharding import PartitionSpec as P

MESH = pl.DeviceIdType.MESH
ZD = 2
GX = 16
GY = 4
F32 = jnp.float32
BF16 = jnp.bfloat16
ROWS = 16
BLK = 256
C0 = 0.7978845608028654
C1 = 0.7978845608028654 * 0.044715


def gelu(x):
    half = 0.5 * x
    return half + half * jnp.tanh(x * (C0 + C1 * (x * x)))


def iota(shape, dim):
    return lax.broadcasted_iota(jnp.int32, shape, dim)


def one_hot(index, ramp):
    row = jnp.broadcast_to(index, (16, index.shape[1])).astype(BF16)
    full = jnp.concatenate([row] * (BLK // 16), axis=0)
    return jnp.where(ramp == full, jnp.ones_like(full), jnp.zeros_like(full))


def kernel(
    slabs,
    feat_h,
    coords_h,
    send_rows_h,
    send_count_h,
    nbr_h,
    counts_h,
    geom_h,
    feat_weight_h,
    bias_one_h,
    hidden_weight_h,
    bias_two_h,
    out_weight_h,
    bias_three_h,
    out,
    feat,
    coords,
    send_rows,
    send_count,
    nbr,
    counts,
    geom_t,
    feat_weight,
    bias_one,
    hidden_weight,
    bias_two,
    out_t,
    bias_three,
    own,
    halo,
    picked,
    side_out,
    side_in,
    table,
    hot,
    grid,
    node,
    stage,
    pack,
    small,
    wide,
    w_pre,
    w_out,
    res,
    rcv,
    in_sem,
    own_send,
    own_recv,
    own_fwd,
    relay_send,
    halo_send,
    halo_recv,
    halo_fwd,
    side_send,
    side_recv,
    res_send,
    res_recv,
):
    s = lax.axis_index("slab")
    c = lax.axis_index("chan")
    chip = c // 2
    core = c % 2
    sib = c + 1 - 2 * core
    upper = c // 4
    inner = (chip == 1) | (chip == 2)
    has_up = s < slabs - 1
    has_down = s > 0
    has_halo = jnp.where(upper == 1, s < slabs - 1, s > 0)
    source_slab = s - 1 + 2 * upper
    points = feat.shape[1]
    send = send_rows.shape[1]
    body = points * 3 // 4
    tail = points - body
    hbody = send * 3 // 4
    htail = send - hbody
    pairs = node.shape[1]

    barrier = pltpu.get_barrier_semaphore()
    for j in range(1, 8):
        pl.semaphore_signal(barrier, inc=1, device_id=(s, (c + j) % 8), device_id_type=MESH)

    @pl.when(has_halo)
    def _():
        for q in range(4):
            pl.semaphore_signal(
                barrier, inc=1, device_id=(source_slab, 2 * q + core), device_id_type=MESH
            )

    loads = [
        pltpu.make_async_copy(a, b, in_sem.at[i])
        for i, (a, b) in enumerate(
            [
                (feat_h, feat),
                (coords_h, coords),
                (send_rows_h, send_rows),
                (send_count_h, send_count),
                (nbr_h, nbr),
                (counts_h, counts),
                (geom_h, geom_t),
                (feat_weight_h, feat_weight),
                (bias_one_h, bias_one),
                (hidden_weight_h, hidden_weight),
                (bias_two_h, bias_two),
                (out_weight_h, out_t),
                (bias_three_h, bias_three),
            ]
        )
    ]
    for load in loads:
        load.start()
    for load in loads[:4]:
        load.wait()

    values = feat[...].astype(F32)
    pack[0:12, :] = values[:, 0:body]
    for g in range(3):
        pack[12:16, g * tail : (g + 1) * tail] = values[4 * g : 4 * g + 4, body:points]
    own[c] = pack[...].astype(BF16)

    stage[0:12, :] = values
    stage[12:15, :] = coords[...].astype(F32)
    stage[15:16, :] = jnp.ones((1, points), F32)
    slot = stage[...].astype(BF16)

    ramp = iota((BLK, 128), 0).astype(F32).astype(BF16)
    pieces = points // BLK
    stacked = jnp.concatenate([slot[:, h * BLK : (h + 1) * BLK] for h in range(pieces)], axis=0)
    lists = []
    for d in range(2):
        idx = send_rows[d : d + 1, :]
        idx = jnp.where(iota((1, send), 1) < send_count[d], idx, -1)
        low = (idx & (BLK - 1)).astype(F32)
        high = lax.shift_right_arithmetic(idx, 8)
        hots = jnp.concatenate(
            [one_hot(low[:, t * 128 : (t + 1) * 128], ramp) for t in range(send // 128)], axis=1
        )
        parts = jnp.dot(stacked, hots, preferred_element_type=F32)
        total = jnp.zeros((ROWS, send), F32)
        for h in range(pieces):
            total = total + jnp.where(high == h, parts[h * ROWS : (h + 1) * ROWS], 0.0)
        pack[0:12, 0:hbody] = total[0:12, 0:hbody]
        for g in range(3):
            pack[12:16, g * htail : (g + 1) * htail] = total[4 * g : 4 * g + 4, hbody:send]
        picked[d] = pack[:, 0:hbody].astype(BF16)
        lists.append(total[12:16, :])
    mine = jnp.where(upper == 1, lists[0], lists[1])
    for j in range(4):
        pack[4 * j : 4 * j + 4, 0:htail] = mine[:, j * htail : (j + 1) * htail]
    side_out[...] = pack[:, 0:htail].astype(BF16)

    pl.semaphore_wait(barrier, 7 + 2 * jnp.where(has_up, 1, 0) + 2 * jnp.where(has_down, 1, 0))

    def remote(src, dst, sem_out, sem_in, target):
        return pltpu.make_async_remote_copy(
            src_ref=src,
            dst_ref=dst,
            send_sem=sem_out,
            recv_sem=sem_in,
            device_id=target,
            device_id_type=MESH,
        )

    def halo_copy(d, q):
        target = (s + 1, 2 * q + core) if d == 1 else (s - 1, 4 + 2 * q + core)
        return remote(picked.at[d], halo.at[c], halo_send.at[d, q], halo_recv.at[c], target)

    def side_copy():
        return remote(
            side_out, side_in, side_send.at[0], side_recv.at[0], (s + 1 - 2 * upper, c)
        )

    def own_copy(j):
        target = sib if j == 0 else 2 * ((chip + j) % 4) + core
        return remote(own.at[c], own.at[c], own_send.at[j], own_recv.at[c], (s, target))

    def own_far(j):
        there = (chip + j) % 4
        return (jnp.abs(there - chip) == 2) & inner

    def when_own(j, act):
        if j == 0:
            act(own_copy(0))
        else:

            @pl.when(jnp.logical_not(own_far(j)))
            def _():
                act(own_copy(j))

    sends_side = jnp.where(upper == 1, s > 0, s < slabs - 1)

    @pl.when(has_up)
    def _():
        for q in range(2):
            halo_copy(1, q).start()

    @pl.when(has_down)
    def _():
        for q in range(2):
            halo_copy(0, q).start()

    @pl.when(sends_side)
    def _():
        side_copy().start()

    for j in range(4):
        when_own(j, lambda copy: copy.start())

    for load in loads[4:]:
        load.wait()
    small[...] = jnp.zeros_like(small)
    small[0:6, 0:80] = geom_t[...].astype(F32)
    small[6:7, 0:80] = bias_one[...]
    small[7:8, 0:80] = bias_two[...]
    lane = iota((96, 128), 1)
    spread = jnp.where(
        (lane // ROWS * 12 + lane % ROWS == iota((96, 128), 0)) & (lane % ROWS < 12), 1.0, 0.0
    )
    small[8:16, :] = jnp.dot(
        jnp.broadcast_to(bias_three[...], (8, 96)),
        spread,
        preferred_element_type=F32,
        precision=lax.Precision.HIGHEST,
    )
    cols = jnp.transpose(small[...])
    spread = spread.astype(BF16)
    w_pre[:, 0:128] = jnp.dot(feat_weight[...], spread, preferred_element_type=F32).astype(BF16)
    lane16 = iota((80, 16), 1)
    w_side = jnp.zeros((80, 16), F32)
    for i in range(3):
        w_side = jnp.where(lane16 == i, cols[0:80, 3 + i : 4 + i], w_side)
    w_pre[:, 128:144] = w_side.astype(BF16)
    small[0:80, :] = jnp.dot(out_t[...], spread, preferred_element_type=F32)
    w_out[...] = jnp.transpose(small[...])[:, 0:80].astype(BF16)
    along_y = ((c % GY).astype(F32) + 0.5) / GY
    along_z = ((2 * s + upper).astype(F32) + 0.5) / (ZD * slabs)
    wide[0:80, :] = jnp.broadcast_to(cols[0:80, 7:8], (80, 128))
    wide[80:208, :] = jnp.broadcast_to(cols[:, 8:9], (128, 128))
    slope = jnp.broadcast_to(cols[0:80, 0:1], (80, 128))
    base = jnp.broadcast_to(
        cols[0:80, 1:2] * along_y + cols[0:80, 2:3] * along_z + cols[0:80, 6:7], (80, 128)
    )
    for n in range(16):
        node[:, n * 128 : (n + 1) * 128] = base + slope * ((n + 0.5) / GX)

    first = pl.multiple_of(c * 16, 16)
    idx = nbr[pl.ds(first, 16), :]
    idx = idx - jnp.where(idx >= points, send * upper, 0)
    slots = iota((1, 128), 1)
    rows = []
    for n in range(16):
        rows.append(jnp.where(slots < counts[first + n], idx[n : n + 1, :], -1))
    lows = [(r & (BLK - 1)).astype(F32) for r in rows]
    highs = [lax.shift_right_arithmetic(r, 8) for r in rows]

    def build(kb, carry):
        at = pl.ds(pl.multiple_of(kb * BLK, BLK), BLK)
        for n in range(16):
            pick = jnp.where(highs[n] == kb, lows[n], -1.0)
            hot[at, n * 128 : (n + 1) * 128] = one_hot(pick, ramp)
        return carry

    lax.fori_loop(0, (points + send) // BLK, build, 0)
    extra = jnp.concatenate(
        [coords[...].astype(F32), jnp.ones((1, points), F32), jnp.zeros((12, points), F32)], axis=0
    )
    table[128:144, 0:points] = extra.astype(BF16)

    def landed(buf, sem, i):
        return remote(buf.at[i], buf.at[i], sem.at[i], sem.at[i], (s, sib))

    def forward(buf, fwd, recv, i, k):
        return remote(buf.at[i], buf.at[i], fwd.at[k], recv.at[i], (s, sib))

    def relay():
        i = 2 * (3 - chip) + core
        return remote(
            own.at[i], own.at[i], relay_send.at[0], own_recv.at[i], (s, 6 * (chip - 1) + core)
        )

    for j in range(1, 4):
        there = jnp.where(inner, (3 - chip + j - 1) % 4, (chip + j) % 4)
        there = jnp.where(inner & (j > 1), jnp.where(j == 2, 0, 3), there)
        i = 2 * there + core
        landed(own, own_recv, i).wait_recv()
        if j == 1:

            @pl.when(inner)
            def _():
                relay().start()

        forward(own, own_fwd, own_recv, i, j - 1).start()
    for j in range(4):
        landed(own, own_recv, 2 * ((chip + j) % 4) + 1 - core).wait_recv()

    table[0:128, 0:body] = own[:, :, 0:body].reshape(128, body)
    for i in range(8):
        rest = own[i].astype(F32)[12:16, :]
        rest = jnp.concatenate(
            [rest[:, g * tail : (g + 1) * tail] for g in range(3)] + [jnp.zeros((4, tail), F32)], axis=0
        )
        table[i * ROWS : (i + 1) * ROWS, body:points] = rest.astype(BF16)
    grid[...] = jnp.dot(table[:, 0:points], hot[0:points, :], preferred_element_type=F32)

    @pl.when(has_halo)
    def _():
        for q in range(4):
            i = 2 * q + core
            landed(halo, halo_recv, i).wait_recv()
            forward(halo, halo_fwd, halo_recv, i, q).start()
        side_copy().wait_recv()
        for q in range(4):
            landed(halo, halo_recv, 2 * q + 1 - core).wait_recv()

    @pl.when(jnp.logical_not(has_halo))
    def _():
        halo[...] = jnp.zeros_like(halo)
        side_in[...] = jnp.zeros_like(side_in)

    table[0:128, points : points + hbody] = halo[...].reshape(128, hbody)
    for i in range(8):
        rest = halo[i].astype(F32)[12:16, :]
        rest = jnp.concatenate(
            [rest[:, g * htail : (g + 1) * htail] for g in range(3)] + [jnp.zeros((4, htail), F32)],
            axis=0,
        )
        table[i * ROWS : (i + 1) * ROWS, points + hbody : points + send] = rest.astype(BF16)
    rest = side_in[...].astype(F32)
    rest = jnp.concatenate([rest[4 * j : 4 * j + 4, :] for j in range(4)], axis=1)
    rest = jnp.concatenate([rest, jnp.zeros((12, send), F32)], axis=0)
    table[128:144, points : points + send] = rest.astype(BF16)

    values = grid[...] + jnp.dot(
        table[:, points : points + send],
        hot[points : points + send, :],
        preferred_element_type=F32,
    )
    pre = jnp.dot(w_pre[...], values.astype(BF16), preferred_element_type=F32)
    h1 = gelu(pre.astype(BF16).astype(F32) + node[...]).astype(BF16)
    h2 = jnp.dot(hidden_weight[...], h1, preferred_element_type=F32)
    h2 = gelu(h2 + jnp.concatenate([wide[0:80, :]] * 16, axis=1)).astype(BF16)
    kappa = jnp.dot(w_out[...], h2, preferred_element_type=F32)
    kappa = kappa + jnp.concatenate([wide[80:208, :]] * 16, axis=1)
    prod = kappa * values[0:128, :]

    lane8 = iota((8, 8, 128), 2)
    lane1 = iota((1, 128), 1)
    low_at = c * 16
    high_at = (c + 4) % 8 * 16
    acc = jnp.zeros((8, 8, 128), F32)
    number = jnp.ones((1, 128), F32)
    for n in range(16):
        at = slice(n * 128, (n + 1) * 128)
        total = jnp.sum(prod[:, at], axis=1, keepdims=True).reshape(8, ROWS, 1)
        acc = jnp.where(
            lane8 == low_at + n,
            total[:, 0:8],
            jnp.where(lane8 == high_at + n, total[:, 8:16], acc),
        )
        used = jnp.sum(values[128:136, at], axis=1, keepdims=True)[3:4]
        number = jnp.where((lane1 == low_at + n) | (lane1 == high_at + n), used, number)
    res[...] = acc / number[None]

    def res_copy(j):
        target = (c + j) % 8
        return remote(res.at[target], rcv.at[c], res_send.at[j - 1], res_recv.at[c], (s, target))

    for j in range(1, 8):
        res_copy(j).start()
    rcv[c] = res[c]

    for j in range(4):
        when_own(j, lambda copy: copy.wait_send())
    for j in range(1, 4):
        forward(own, own_fwd, own_recv, c, j - 1).wait_send()

    @pl.when(inner)
    def _():
        relay().wait_send()

    @pl.when(has_up)
    def _():
        for q in range(2):
            halo_copy(1, q).wait_send()

    @pl.when(has_down)
    def _():
        for q in range(2):
            halo_copy(0, q).wait_send()

    @pl.when(sends_side)
    def _():
        side_copy().wait_send()

    @pl.when(has_halo)
    def _():
        for q in range(4):
            forward(halo, halo_fwd, halo_recv, 2 * q + core, q).wait_send()

    for j in range(1, 8):
        landed(rcv, res_recv, (c + j) % 8).wait_recv()
    for j in range(1, 8):
        res_copy(j).wait_send()
    group = iota((8, 128), 1) // 16
    lower_rows = jnp.zeros((8, 128), F32)
    upper_rows = jnp.zeros((8, 128), F32)
    for i in range(8):
        lower_rows = jnp.where(group == i, rcv[i], lower_rows)
        upper_rows = jnp.where(group == (i + 4) % 8, rcv[i], upper_rows)
    out[0:8, :] = lower_rows
    out[8:12, :] = pltpu.roll(upper_rows, 64, 1)[0:4, :]


def shards(
    slabs,
    features,
    coords,
    send_rows,
    send_count,
    neighbours,
    neighbour_count,
    geom_weight,
    feat_weight,
    bias_one,
    hidden_weight,
    bias_two,
    out_weight,
    bias_three,
):
    points = features.shape[1]
    send = send_rows.shape[1]
    pairs = 16 * neighbours.shape[1]
    args = (
        features,
        coords,
        send_rows,
        send_count.reshape(2),
        neighbours,
        neighbour_count,
        geom_weight.T,
        feat_weight,
        bias_one.reshape(1, -1),
        hidden_weight,
        bias_two.reshape(1, -1),
        out_weight.T,
        bias_three.reshape(1, -1),
    )
    dma = pltpu.SemaphoreType.DMA
    held = [
        (pltpu.SMEM if i in (3, 5) else pltpu.VMEM)(a.shape, a.dtype) for i, a in enumerate(args)
    ]
    return pl.pallas_call(
        functools.partial(kernel, slabs),
        out_shape=jax.ShapeDtypeStruct((12, 128), F32),
        in_specs=[pl.BlockSpec(memory_space=pl.ANY)] * len(args),
        out_specs=pl.BlockSpec(memory_space=pltpu.VMEM),
        scratch_shapes=held
        + [
            pltpu.VMEM((8, ROWS, points * 3 // 4), BF16),
            pltpu.VMEM((8, ROWS, send * 3 // 4), BF16),
            pltpu.VMEM((2, ROWS, send * 3 // 4), BF16),
            pltpu.VMEM((ROWS, send // 4), BF16),
            pltpu.VMEM((ROWS, send // 4), BF16),
            pltpu.VMEM((9 * ROWS, points + send), BF16),
            pltpu.VMEM((points + send, pairs), BF16),
            pltpu.VMEM((9 * ROWS, pairs), F32),
            pltpu.VMEM((80, pairs), F32),
            pltpu.VMEM((ROWS, points), F32),
            pltpu.VMEM((ROWS, points * 3 // 4), F32),
            pltpu.VMEM((128, 128), F32),
            pltpu.VMEM((208, 128), F32),
            pltpu.VMEM((80, 9 * ROWS), BF16),
            pltpu.VMEM((128, 80), BF16),
            pltpu.VMEM((8, 8, 128), F32),
            pltpu.VMEM((8, 8, 128), F32),
            dma((len(args),)),
            dma((4,)),
            dma((8,)),
            dma((3,)),
            dma((1,)),
            dma((2, 2)),
            dma((8,)),
            dma((4,)),
            dma((1,)),
            dma((1,)),
            dma((7,)),
            dma((8,)),
        ],
        compiler_params=pltpu.CompilerParams(
            collective_id=0, has_side_effects=True, vmem_limit_bytes=60 * 2**20
        ),
    )(*args)


def solution(mesh):
    placed = (
        P("chan", "slab"),
        P(None, "slab"),
        P(None, "slab"),
        P(None, "slab"),
        P("slab", None),
        P("slab"),
        P(),
        P(),
        P(),
        P(),
        P(),
        P(),
        P(),
    )
    return jax.shard_map(
        functools.partial(shards, mesh.shape["slab"]),
        mesh=mesh,
        in_specs=placed,
        out_specs=P("chan", "slab"),
        check_vma=False,
    )
```

time: 37.9 us -> 29.3 us (0.77)
  Pallas kernels: 36.4 us -> 27.8 us
    pallas_call x1, Pallas kernels: 36.4 us -> 27.8 us  [shards(): pl.pallas_call(functools.partial(kernel, slabs), out_shape=jax.ShapeDtype...]
where the time goes in v2:
time: 29.3 us; the launch traced here: 29.1 us
  Pallas kernels  27.8 us (95%)
  local copies, waits for them, and re-layouts  1.3 us (4%)
    pallas_call x1, Pallas kernels, shards(): pl.pallas_call(functools.partial(kernel, slabs), out_shape=jax.ShapeDtype...  27.8 us
    unnamed x1, local copies, waits for them, and re-layouts  1.3 us

profile of v2, /device:TPU:31, one launch (start us, length us, event | category | flops | bytes accessed | tf_op | source)
XLA Modules:
  0.0 29.1 jit_solution(16283908359676699852)
XLA Ops:
  0.0 27.8 %shard_map.127 = f32[12,128]{1,0:T(8,128)} custom-call(bf16[12,2048]{1,0:T(8,128)(2,1)} %feat_h.1, bf16[3,2048]{1,0:T(4,128)(2,1)} %coords_h.1, s32[2,1024]{1,0:T(2,128)} %send_rows_h.1, s32[2]{0:T(128)} %bitcast.8, s32[128,128]{1,0:T(8,128)} %nbr_h.1, s32[128]{0:T(128)} %counts_h.1, bf16[6,80]{1,0:T(8,128)(2,1)} %bitcast.7, bf16[80,96]{1,0:T(8,128)(2,1)} %feat_weight_h.1, ...), custom_call_target="tpu_custom_call" | custom-call | tf_op jit(solution)/shard_map/pallas_call | solution.py:488
  27.8 1.3 %copy.15 = f32[12,128]{1,0:T(8,128)} copy(f32[12,128]{1,0:T(8,128)} %shard_map.127) | data formatting | bytes 12288

commit v3 on v2

--- a/solution.py
+++ b/solution.py
@@ -84,7 +84,6 @@
     own_send,
     own_recv,
     own_fwd,
-    relay_send,
     halo_send,
     halo_recv,
     halo_fwd,
@@ -98,12 +97,16 @@
     chip = c // 2
     core = c % 2
     sib = c + 1 - 2 * core
-    upper = c // 4
-    inner = (chip == 1) | (chip == 2)
+    ends = 1 - (chip + 1) // 2 % 2
+    half = s * 2 // slabs
+    upper = jnp.where(half == 0, ends, 1 - ends)
+    rank = 2 * jnp.where(ends == 1, chip // 3, chip - 1) + core
+    place = 4 * upper + rank
     has_up = s < slabs - 1
     has_down = s > 0
     has_halo = jnp.where(upper == 1, s < slabs - 1, s > 0)
     source_slab = s - 1 + 2 * upper
+    distant = source_slab * 2 // slabs != half
     points = feat.shape[1]
     send = send_rows.shape[1]
     body = points * 3 // 4
@@ -162,7 +165,6 @@
     ramp = iota((BLK, 128), 0).astype(F32).astype(BF16)
     pieces = points // BLK
     stacked = jnp.concatenate([slot[:, h * BLK : (h + 1) * BLK] for h in range(pieces)], axis=0)
-    lists = []
     for d in range(2):
         idx = send_rows[d : d + 1, :]
         idx = jnp.where(iota((1, send), 1) < send_count[d], idx, -1)
@@ -179,11 +181,9 @@
         for g in range(3):
             pack[12:16, g * htail : (g + 1) * htail] = total[4 * g : 4 * g + 4, hbody:send]
         picked[d] = pack[:, 0:hbody].astype(BF16)
-        lists.append(total[12:16, :])
-    mine = jnp.where(upper == 1, lists[0], lists[1])
-    for j in range(4):
-        pack[4 * j : 4 * j + 4, 0:htail] = mine[:, j * htail : (j + 1) * htail]
-    side_out[...] = pack[:, 0:htail].astype(BF16)
+        for j in range(4):
+            pack[4 * j : 4 * j + 4, 0:htail] = total[12:16, j * htail : (j + 1) * htail]
+        side_out[d] = pack[:, 0:htail].astype(BF16)
 
     pl.semaphore_wait(barrier, 7 + 2 * jnp.where(has_up, 1, 0) + 2 * jnp.where(has_down, 1, 0))
 
@@ -197,50 +197,44 @@
             device_id_type=MESH,
         )
 
+    def reached(d):
+        if d == 1:
+            return jnp.where(s + 1 < slabs // 2, 0, 1)
+        return jnp.where(s - 1 < slabs // 2, 1, 0)
+
     def halo_copy(d, q):
-        target = (s + 1, 2 * q + core) if d == 1 else (s - 1, 4 + 2 * q + core)
+        there = jnp.where(reached(d) == 1, 3 * q, 1 + q)
+        target = (s - 1 + 2 * d, 2 * there + core)
         return remote(picked.at[d], halo.at[c], halo_send.at[d, q], halo_recv.at[c], target)
 
-    def side_copy():
+    def side_copy(d):
         return remote(
-            side_out, side_in, side_send.at[0], side_recv.at[0], (s + 1 - 2 * upper, c)
-        )
+            side_out.at[d], side_in, side_send.at[d], side_recv.at[0], (s - 1 + 2 * d, c)
+        )
+
+    def there_of(j):
+        up = j - 1 + jnp.where(chip <= j - 1, 1, 0)
+        down = 4 - j - jnp.where(3 - chip <= j - 1, 1, 0)
+        return jnp.where(chip < 2, down, up)
 
     def own_copy(j):
-        target = sib if j == 0 else 2 * ((chip + j) % 4) + core
+        target = sib if j == 0 else 2 * there_of(j) + core
         return remote(own.at[c], own.at[c], own_send.at[j], own_recv.at[c], (s, target))
 
-    def own_far(j):
-        there = (chip + j) % 4
-        return (jnp.abs(there - chip) == 2) & inner
-
-    def when_own(j, act):
-        if j == 0:
-            act(own_copy(0))
-        else:
-
-            @pl.when(jnp.logical_not(own_far(j)))
+    def when_list(d, act):
+        @pl.when(has_up if d == 1 else has_down)
+        def _():
+            for q in range(2):
+                act(halo_copy(d, q))
+
+            @pl.when(reached(d) == ends)
             def _():
-                act(own_copy(j))
-
-    sends_side = jnp.where(upper == 1, s > 0, s < slabs - 1)
-
-    @pl.when(has_up)
-    def _():
-        for q in range(2):
-            halo_copy(1, q).start()
-
-    @pl.when(has_down)
-    def _():
-        for q in range(2):
-            halo_copy(0, q).start()
-
-    @pl.when(sends_side)
-    def _():
-        side_copy().start()
-
-    for j in range(4):
-        when_own(j, lambda copy: copy.start())
+                act(side_copy(d))
+
+    for d in (1, 0):
+        when_list(d, lambda copy: copy.start())
+    for j in (1, 2, 3, 0):
+        own_copy(j).start()
 
     for load in loads[4:]:
         load.wait()
@@ -268,7 +262,7 @@
     w_pre[:, 128:144] = w_side.astype(BF16)
     small[0:80, :] = jnp.dot(out_t[...], spread, preferred_element_type=F32)
     w_out[...] = jnp.transpose(small[...])[:, 0:80].astype(BF16)
-    along_y = ((c % GY).astype(F32) + 0.5) / GY
+    along_y = ((rank % GY).astype(F32) + 0.5) / GY
     along_z = ((2 * s + upper).astype(F32) + 0.5) / (ZD * slabs)
     wide[0:80, :] = jnp.broadcast_to(cols[0:80, 7:8], (80, 128))
     wide[80:208, :] = jnp.broadcast_to(cols[:, 8:9], (128, 128))
@@ -279,7 +273,7 @@
     for n in range(16):
         node[:, n * 128 : (n + 1) * 128] = base + slope * ((n + 0.5) / GX)
 
-    first = pl.multiple_of(c * 16, 16)
+    first = pl.multiple_of(place * 16, 16)
     idx = nbr[pl.ds(first, 16), :]
     idx = idx - jnp.where(idx >= points, send * upper, 0)
     slots = iota((1, 128), 1)
@@ -308,24 +302,21 @@
     def forward(buf, fwd, recv, i, k):
         return remote(buf.at[i], buf.at[i], fwd.at[k], recv.at[i], (s, sib))
 
-    def relay():
-        i = 2 * (3 - chip) + core
-        return remote(
-            own.at[i], own.at[i], relay_send.at[0], own_recv.at[i], (s, 6 * (chip - 1) + core)
-        )
+    def take_halo():
+        for q in range(4):
+            i = 2 * q + core
+            landed(halo, halo_recv, i).wait_recv()
+            forward(halo, halo_fwd, halo_recv, i, q).start()
 
     for j in range(1, 4):
-        there = jnp.where(inner, (3 - chip + j - 1) % 4, (chip + j) % 4)
-        there = jnp.where(inner & (j > 1), jnp.where(j == 2, 0, 3), there)
-        i = 2 * there + core
+        i = 2 * ((chip + j) % 4) + core
         landed(own, own_recv, i).wait_recv()
-        if j == 1:
-
-            @pl.when(inner)
-            def _():
-                relay().start()
-
         forward(own, own_fwd, own_recv, i, j - 1).start()
+
+    @pl.when(has_halo & jnp.logical_not(distant))
+    def _():
+        take_halo()
+
     for j in range(4):
         landed(own, own_recv, 2 * ((chip + j) % 4) + 1 - core).wait_recv()
 
@@ -338,13 +329,13 @@
         table[i * ROWS : (i + 1) * ROWS, body:points] = rest.astype(BF16)
     grid[...] = jnp.dot(table[:, 0:points], hot[0:points, :], preferred_element_type=F32)
 
+    @pl.when(has_halo & distant)
+    def _():
+        take_halo()
+
     @pl.when(has_halo)
     def _():
-        for q in range(4):
-            i = 2 * q + core
-            landed(halo, halo_recv, i).wait_recv()
-            forward(halo, halo_fwd, halo_recv, i, q).start()
-        side_copy().wait_recv()
+        side_copy(0).wait_recv()
         for q in range(4):
             landed(halo, halo_recv, 2 * q + 1 - core).wait_recv()
 
@@ -381,8 +372,8 @@
 
     lane8 = iota((8, 8, 128), 2)
     lane1 = iota((1, 128), 1)
-    low_at = c * 16
-    high_at = (c + 4) % 8 * 16
+    low_at = place * 16
+    high_at = (place + 4) % 8 * 16
     acc = jnp.zeros((8, 8, 128), F32)
     number = jnp.ones((1, 128), F32)
     for n in range(16):
@@ -399,34 +390,20 @@
 
     def res_copy(j):
         target = (c + j) % 8
-        return remote(res.at[target], rcv.at[c], res_send.at[j - 1], res_recv.at[c], (s, target))
+        return remote(
+            res.at[target], rcv.at[place], res_send.at[j - 1], res_recv.at[place], (s, target)
+        )
 
     for j in range(1, 8):
         res_copy(j).start()
-    rcv[c] = res[c]
+    rcv[place] = res[c]
 
     for j in range(4):
-        when_own(j, lambda copy: copy.wait_send())
+        own_copy(j).wait_send()
     for j in range(1, 4):
         forward(own, own_fwd, own_recv, c, j - 1).wait_send()
-
-    @pl.when(inner)
-    def _():
-        relay().wait_send()
-
-    @pl.when(has_up)
-    def _():
-        for q in range(2):
-            halo_copy(1, q).wait_send()
-
-    @pl.when(has_down)
-    def _():
-        for q in range(2):
-            halo_copy(0, q).wait_send()
-
-    @pl.when(sends_side)
-    def _():
-        side_copy().wait_send()
+    for d in (1, 0):
+        when_list(d, lambda copy: copy.wait_send())
 
     @pl.when(has_halo)
     def _():
@@ -434,7 +411,7 @@
             forward(halo, halo_fwd, halo_recv, 2 * q + core, q).wait_send()
 
     for j in range(1, 8):
-        landed(rcv, res_recv, (c + j) % 8).wait_recv()
+        landed(rcv, res_recv, (place + j) % 8).wait_recv()
     for j in range(1, 8):
         res_copy(j).wait_send()
     group = iota((8, 128), 1) // 16
@@ -495,7 +472,7 @@
             pltpu.VMEM((8, ROWS, points * 3 // 4), BF16),
             pltpu.VMEM((8, ROWS, send * 3 // 4), BF16),
             pltpu.VMEM((2, ROWS, send * 3 // 4), BF16),
-            pltpu.VMEM((ROWS, send // 4), BF16),
+            pltpu.VMEM((2, ROWS, send // 4), BF16),
             pltpu.VMEM((ROWS, send // 4), BF16),
             pltpu.VMEM((9 * ROWS, points + send), BF16),
             pltpu.VMEM((points + send, pairs), BF16),
@@ -513,11 +490,10 @@
             dma((4,)),
             dma((8,)),
             dma((3,)),
-            dma((1,)),
             dma((2, 2)),
             dma((8,)),
             dma((4,)),
-            dma((1,)),
+            dma((2,)),
             dma((1,)),
             dma((7,)),
             dma((8,)),

time: 29.3 us -> 26.5 us (0.904)
  Pallas kernels: 27.8 us -> 25 us
    pallas_call x1, Pallas kernels: 27.8 us -> 25 us  [shards(): pl.pallas_call(functools.partial(kernel, slabs), out_shape=jax.ShapeDtype...]
where the time goes in v3:
time: 26.5 us; the launch traced here: 26.3 us
  Pallas kernels  25 us (94%)
  local copies, waits for them, and re-layouts  1.3 us (5%)
    pallas_call x1, Pallas kernels, shards(): pl.pallas_call(functools.partial(kernel, slabs), out_shape=jax.ShapeDtype...  25 us
    unnamed x1, local copies, waits for them, and re-layouts  1.3 us

profile of v3, /device:TPU:31, one launch (start us, length us, event | category | flops | bytes accessed | tf_op | source)
XLA Modules:
  0.0 26.3 jit_solution(16466242023474695607)
XLA Ops:
  0.0 25.0 %shard_map.127 = f32[12,128]{1,0:T(8,128)} custom-call(bf16[12,2048]{1,0:T(8,128)(2,1)} %feat_h.1, bf16[3,2048]{1,0:T(4,128)(2,1)} %coords_h.1, s32[2,1024]{1,0:T(2,128)} %send_rows_h.1, s32[2]{0:T(128)} %bitcast.8, s32[128,128]{1,0:T(8,128)} %nbr_h.1, s32[128]{0:T(128)} %counts_h.1, bf16[6,80]{1,0:T(8,128)(2,1)} %bitcast.7, bf16[80,96]{1,0:T(8,128)(2,1)} %feat_weight_h.1, ...), custom_call_target="tpu_custom_call" | custom-call | tf_op jit(solution)/shard_map/pallas_call | solution.py:465
  25.0 1.3 %copy.15 = f32[12,128]{1,0:T(8,128)} copy(f32[12,128]{1,0:T(8,128)} %shard_map.127) | data formatting | bytes 12288

commit v4 on v3

--- a/solution.py
+++ b/solution.py
@@ -66,6 +66,7 @@
     own,
     halo,
     picked,
+    passing,
     side_out,
     side_in,
     table,
@@ -85,8 +86,11 @@
     own_recv,
     own_fwd,
     halo_send,
+    far_send,
     halo_recv,
     halo_fwd,
+    pass_recv,
+    z_send,
     side_send,
     side_recv,
     res_send,
@@ -97,16 +101,23 @@
     chip = c // 2
     core = c % 2
     sib = c + 1 - 2 * core
-    ends = 1 - (chip + 1) // 2 % 2
+    front = 1 - chip // 2
     half = s * 2 // slabs
-    upper = jnp.where(half == 0, ends, 1 - ends)
-    rank = 2 * jnp.where(ends == 1, chip // 3, chip - 1) + core
+    upper = jnp.where(half == 0, front, 1 - front)
+    rank = 2 * (chip % 2) + core
     place = 4 * upper + rank
+    early = (half == 0) & (front == 1)
     has_up = s < slabs - 1
     has_down = s > 0
+    has = (has_down, has_up)
     has_halo = jnp.where(upper == 1, s < slabs - 1, s > 0)
-    source_slab = s - 1 + 2 * upper
-    distant = source_slab * 2 // slabs != half
+    distant = (s == slabs // 2, s == slabs // 2 - 1)
+    near = tuple(has[d] & jnp.logical_not(distant[d]) for d in range(2))
+    plane_far = jnp.where(upper == 1, s == slabs // 2 - 1, s == slabs // 2)
+    plane_near = has_halo & jnp.logical_not(plane_far)
+    flip = 2 * (3 - chip) + core
+    beside = 2 * (chip + 1 - 2 * (chip % 2)) + core
+
     points = feat.shape[1]
     send = send_rows.shape[1]
     body = points * 3 // 4
@@ -119,12 +130,23 @@
     for j in range(1, 8):
         pl.semaphore_signal(barrier, inc=1, device_id=(s, (c + j) % 8), device_id_type=MESH)
 
-    @pl.when(has_halo)
-    def _():
-        for q in range(4):
+    for d in range(2):
+
+        @pl.when(near[d])
+        def _():
             pl.semaphore_signal(
-                barrier, inc=1, device_id=(source_slab, 2 * q + core), device_id_type=MESH
+                barrier, inc=1, device_id=(s - 1 + 2 * d, c), device_id_type=MESH
             )
+
+        @pl.when(distant[d] & (front == 1))
+        def _():
+            for q in range(4):
+                pl.semaphore_signal(
+                    barrier,
+                    inc=1,
+                    device_id=(s - 1 + 2 * d, 2 * q + core),
+                    device_id_type=MESH,
+                )
 
     loads = [
         pltpu.make_async_copy(a, b, in_sem.at[i])
@@ -148,7 +170,7 @@
     ]
     for load in loads:
         load.start()
-    for load in loads[:4]:
+    for load in loads[:6]:
         load.wait()
 
     values = feat[...].astype(F32)
@@ -185,7 +207,31 @@
             pack[4 * j : 4 * j + 4, 0:htail] = total[12:16, j * htail : (j + 1) * htail]
         side_out[d] = pack[:, 0:htail].astype(BF16)
 
-    pl.semaphore_wait(barrier, 7 + 2 * jnp.where(has_up, 1, 0) + 2 * jnp.where(has_down, 1, 0))
+    first = pl.multiple_of(place * 16, 16)
+    idx = nbr[pl.ds(first, 16), :]
+    idx = idx - jnp.where(idx >= points, send * upper, 0)
+    slots = iota((1, 128), 1)
+    rows = []
+    for n in range(16):
+        rows.append(jnp.where(slots < counts[first + n], idx[n : n + 1, :], -1))
+    lows = [(r & (BLK - 1)).astype(F32) for r in rows]
+    highs = [lax.shift_right_arithmetic(r, 8) for r in rows]
+
+    def build(kb, carry):
+        at = pl.ds(pl.multiple_of(kb * BLK, BLK), BLK)
+        for n in range(16):
+            pick = jnp.where(highs[n] == kb, lows[n], -1.0)
+            hot[at, n * 128 : (n + 1) * 128] = one_hot(pick, ramp)
+        return carry
+
+    steps = (points + send) // BLK
+
+    @pl.when(early)
+    def _():
+        lax.fori_loop(0, steps, build, 0)
+
+    others = [jnp.where(has[d], jnp.where(distant[d], 2, 1), 0) for d in range(2)]
+    pl.semaphore_wait(barrier, 7 + others[0] + others[1])
 
     def remote(src, dst, sem_out, sem_in, target):
         return pltpu.make_async_remote_copy(
@@ -197,19 +243,27 @@
             device_id_type=MESH,
         )
 
-    def reached(d):
-        if d == 1:
-            return jnp.where(s + 1 < slabs // 2, 0, 1)
-        return jnp.where(s - 1 < slabs // 2, 1, 0)
-
-    def halo_copy(d, q):
-        there = jnp.where(reached(d) == 1, 3 * q, 1 + q)
-        target = (s - 1 + 2 * d, 2 * there + core)
-        return remote(picked.at[d], halo.at[c], halo_send.at[d, q], halo_recv.at[c], target)
-
-    def side_copy(d):
+    def list_copy(d, direct):
         return remote(
-            side_out.at[d], side_in, side_send.at[d], side_recv.at[0], (s - 1 + 2 * d, c)
+            picked.at[d],
+            halo.at[c] if direct else passing,
+            halo_send.at[d],
+            halo_recv.at[c] if direct else pass_recv.at[0],
+            (s - 1 + 2 * d, c),
+        )
+
+    def far_copy(d, q):
+        return remote(
+            picked.at[d],
+            halo.at[c],
+            far_send.at[q],
+            halo_recv.at[c],
+            (s - 1 + 2 * d, 2 * q + core),
+        )
+
+    def side_copy(d, target):
+        return remote(
+            side_out.at[d], side_in, side_send.at[d], side_recv.at[0], (s - 1 + 2 * d, target)
         )
 
     def there_of(j):
@@ -222,21 +276,73 @@
         return remote(own.at[c], own.at[c], own_send.at[j], own_recv.at[c], (s, target))
 
     def when_list(d, act):
-        @pl.when(has_up if d == 1 else has_down)
+        @pl.when(distant[d])
         def _():
             for q in range(2):
-                act(halo_copy(d, q))
-
-            @pl.when(reached(d) == ends)
+                act(far_copy(d, q))
+
+            @pl.when(front == 0)
             def _():
-                act(side_copy(d))
+                act(side_copy(d, flip))
+
+        @pl.when(near[d] & (upper != d))
+        def _():
+            act(list_copy(d, True))
+            act(side_copy(d, c))
+
+        @pl.when(near[d] & (upper == d))
+        def _():
+            act(list_copy(d, False))
 
     for d in (1, 0):
         when_list(d, lambda copy: copy.start())
     for j in (1, 2, 3, 0):
         own_copy(j).start()
 
-    for load in loads[4:]:
+    def landed(buf, sem, i):
+        return remote(buf.at[i], buf.at[i], sem.at[i], sem.at[i], (s, sib))
+
+    def forward(buf, fwd, recv, i, k):
+        return remote(buf.at[i], buf.at[i], fwd.at[k], recv.at[i], (s, sib))
+
+    def same_plane():
+        return remote(halo.at[c], halo.at[c], z_send.at[0], halo_recv.at[c], (s, beside))
+
+    def other_plane(q):
+        return remote(
+            passing,
+            halo.at[c],
+            z_send.at[1 + q],
+            halo_recv.at[c],
+            (s, 2 * (2 * front + q) + core),
+        )
+
+    def when_pass(d, act):
+        @pl.when(near[d] & (upper == d))
+        def _():
+            act(same_plane())
+
+        @pl.when(near[d] & (upper != d))
+        def _():
+            for q in range(2):
+                act(other_plane(q))
+
+    def pass_near():
+        for d in range(2):
+
+            @pl.when(near[d] & (upper == d))
+            def _():
+                landed(halo, halo_recv, c).wait_recv()
+                same_plane().start()
+                forward(halo, halo_fwd, halo_recv, c, 0).start()
+
+            @pl.when(near[d] & (upper != d))
+            def _():
+                remote(passing, passing, pass_recv.at[0], pass_recv.at[0], (s, sib)).wait_recv()
+                for q in range(2):
+                    other_plane(q).start()
+
+    for load in loads[6:]:
         load.wait()
     small[...] = jnp.zeros_like(small)
     small[0:6, 0:80] = geom_t[...].astype(F32)
@@ -273,49 +379,32 @@
     for n in range(16):
         node[:, n * 128 : (n + 1) * 128] = base + slope * ((n + 0.5) / GX)
 
-    first = pl.multiple_of(place * 16, 16)
-    idx = nbr[pl.ds(first, 16), :]
-    idx = idx - jnp.where(idx >= points, send * upper, 0)
-    slots = iota((1, 128), 1)
-    rows = []
-    for n in range(16):
-        rows.append(jnp.where(slots < counts[first + n], idx[n : n + 1, :], -1))
-    lows = [(r & (BLK - 1)).astype(F32) for r in rows]
-    highs = [lax.shift_right_arithmetic(r, 8) for r in rows]
-
-    def build(kb, carry):
-        at = pl.ds(pl.multiple_of(kb * BLK, BLK), BLK)
-        for n in range(16):
-            pick = jnp.where(highs[n] == kb, lows[n], -1.0)
-            hot[at, n * 128 : (n + 1) * 128] = one_hot(pick, ramp)
-        return carry
-
-    lax.fori_loop(0, (points + send) // BLK, build, 0)
+    @pl.when(jnp.logical_not(early))
+    def _():
+        lax.fori_loop(0, steps // 2, build, 0)
+
+    pass_near()
+
+    @pl.when(jnp.logical_not(early))
+    def _():
+        lax.fori_loop(steps // 2, steps, build, 0)
+
     extra = jnp.concatenate(
         [coords[...].astype(F32), jnp.ones((1, points), F32), jnp.zeros((12, points), F32)], axis=0
     )
     table[128:144, 0:points] = extra.astype(BF16)
-
-    def landed(buf, sem, i):
-        return remote(buf.at[i], buf.at[i], sem.at[i], sem.at[i], (s, sib))
-
-    def forward(buf, fwd, recv, i, k):
-        return remote(buf.at[i], buf.at[i], fwd.at[k], recv.at[i], (s, sib))
-
-    def take_halo():
-        for q in range(4):
-            i = 2 * q + core
-            landed(halo, halo_recv, i).wait_recv()
-            forward(halo, halo_fwd, halo_recv, i, q).start()
 
     for j in range(1, 4):
         i = 2 * ((chip + j) % 4) + core
         landed(own, own_recv, i).wait_recv()
         forward(own, own_fwd, own_recv, i, j - 1).start()
 
-    @pl.when(has_halo & jnp.logical_not(distant))
-    def _():
-        take_halo()
+    @pl.when(plane_near)
+    def _():
+        for q in range(1, 4):
+            i = 2 * ((chip + q) % 4) + core
+            landed(halo, halo_recv, i).wait_recv()
+            forward(halo, halo_fwd, halo_recv, i, q).start()
 
     for j in range(4):
         landed(own, own_recv, 2 * ((chip + j) % 4) + 1 - core).wait_recv()
@@ -329,13 +418,16 @@
         table[i * ROWS : (i + 1) * ROWS, body:points] = rest.astype(BF16)
     grid[...] = jnp.dot(table[:, 0:points], hot[0:points, :], preferred_element_type=F32)
 
-    @pl.when(has_halo & distant)
-    def _():
-        take_halo()
+    @pl.when(plane_far)
+    def _():
+        for q in range(4):
+            i = 2 * (3 - q) + core
+            landed(halo, halo_recv, i).wait_recv()
+            forward(halo, halo_fwd, halo_recv, i, q).start()
 
     @pl.when(has_halo)
     def _():
-        side_copy(0).wait_recv()
+        side_copy(0, c).wait_recv()
         for q in range(4):
             landed(halo, halo_recv, 2 * q + 1 - core).wait_recv()
 
@@ -404,6 +496,9 @@
         forward(own, own_fwd, own_recv, c, j - 1).wait_send()
     for d in (1, 0):
         when_list(d, lambda copy: copy.wait_send())
+
+    for d in range(2):
+        when_pass(d, lambda copy: copy.wait_send())
 
     @pl.when(has_halo)
     def _():
@@ -472,6 +567,7 @@
             pltpu.VMEM((8, ROWS, points * 3 // 4), BF16),
             pltpu.VMEM((8, ROWS, send * 3 // 4), BF16),
             pltpu.VMEM((2, ROWS, send * 3 // 4), BF16),
+            pltpu.VMEM((ROWS, send * 3 // 4), BF16),
             pltpu.VMEM((2, ROWS, send // 4), BF16),
             pltpu.VMEM((ROWS, send // 4), BF16),
             pltpu.VMEM((9 * ROWS, points + send), BF16),
@@ -490,9 +586,12 @@
             dma((4,)),
             dma((8,)),
             dma((3,)),
-            dma((2, 2)),
+            dma((2,)),
+            dma((2,)),
             dma((8,)),
             dma((4,)),
+            dma((1,)),
+            dma((3,)),
             dma((2,)),
             dma((1,)),
             dma((7,)),

time: 26.5 us -> 25.5 us (0.962)
  Pallas kernels: 25 us -> 24.1 us
    pallas_call x1, Pallas kernels: 25 us -> 24.1 us  [shards(): pl.pallas_call(functools.partial(kernel, slabs), out_shape=jax.ShapeDtype...]
where the time goes in v4:
time: 25.5 us; the launch traced here: 25.4 us
  Pallas kernels  24.1 us (95%)
  local copies, waits for them, and re-layouts  1.3 us (5%)
    pallas_call x1, Pallas kernels, shards(): pl.pallas_call(functools.partial(kernel, slabs), out_shape=jax.ShapeDtype...  24.1 us
    unnamed x1, local copies, waits for them, and re-layouts  1.3 us

profile of v4, /device:TPU:31, one launch (start us, length us, event | category | flops | bytes accessed | tf_op | source)
XLA Modules:
  0.0 25.4 jit_solution(16221528977792088121)
XLA Ops:
  0.0 24.1 %shard_map.127 = f32[12,128]{1,0:T(8,128)} custom-call(bf16[12,2048]{1,0:T(8,128)(2,1)} %feat_h.1, bf16[3,2048]{1,0:T(4,128)(2,1)} %coords_h.1, s32[2,1024]{1,0:T(2,128)} %send_rows_h.1, s32[2]{0:T(128)} %bitcast.8, s32[128,128]{1,0:T(8,128)} %nbr_h.1, s32[128]{0:T(128)} %counts_h.1, bf16[6,80]{1,0:T(8,128)(2,1)} %bitcast.7, bf16[80,96]{1,0:T(8,128)(2,1)} %feat_weight_h.1, ...), custom_call_target="tpu_custom_call" | custom-call | tf_op jit(solution)/shard_map/pallas_call | solution.py:560
  24.1 1.3 %copy.15 = f32[12,128]{1,0:T(8,128)} copy(f32[12,128]{1,0:T(8,128)} %shard_map.127) | data formatting | bytes 12288

commit v5 on v4

--- a/solution.py
+++ b/solution.py
@@ -67,6 +67,7 @@
     halo,
     picked,
     passing,
+    gated,
     side_out,
     side_in,
     table,
@@ -91,6 +92,8 @@
     halo_fwd,
     pass_recv,
     z_send,
+    gate_recv,
+    gate_send,
     side_send,
     side_recv,
     res_send,
@@ -138,15 +141,21 @@
                 barrier, inc=1, device_id=(s - 1 + 2 * d, c), device_id_type=MESH
             )
 
-        @pl.when(distant[d] & (front == 1))
-        def _():
-            for q in range(4):
-                pl.semaphore_signal(
-                    barrier,
-                    inc=1,
-                    device_id=(s - 1 + 2 * d, 2 * q + core),
-                    device_id_type=MESH,
-                )
+    def greet(there):
+        pl.semaphore_signal(barrier, inc=1, device_id=there, device_id_type=MESH)
+
+    @pl.when(distant[1] & (front == 1))
+    def _():
+        for q in range(4):
+            greet((s + 1, 2 * q + core))
+
+    @pl.when(distant[0] & (chip != 2))
+    def _():
+        greet((s - 1, 2 * jnp.where(chip == 3, 0, 3) + core))
+
+    @pl.when(distant[0] & ((chip == 0) | (chip == 3)))
+    def _():
+        greet((s - 1, 2 * jnp.where(chip == 3, 1, 2) + core))
 
     loads = [
         pltpu.make_async_copy(a, b, in_sem.at[i])
@@ -230,7 +239,8 @@
     def _():
         lax.fori_loop(0, steps, build, 0)
 
-    others = [jnp.where(has[d], jnp.where(distant[d], 2, 1), 0) for d in range(2)]
+    far_count = (2, jnp.where(chip == 3, 2, 1))
+    others = [jnp.where(has[d], jnp.where(distant[d], far_count[d], 1), 0) for d in range(2)]
     pl.semaphore_wait(barrier, 7 + others[0] + others[1])
 
     def remote(src, dst, sem_out, sem_in, target):
@@ -252,18 +262,26 @@
             (s - 1 + 2 * d, c),
         )
 
-    def far_copy(d, q):
+    def far_down(q):
         return remote(
-            picked.at[d],
-            halo.at[c],
-            far_send.at[q],
-            halo_recv.at[c],
-            (s - 1 + 2 * d, 2 * q + core),
-        )
-
-    def side_copy(d, target):
+            picked.at[0], halo.at[c], far_send.at[q], halo_recv.at[c], (s - 1, 2 * q + core)
+        )
+
+    def far_up():
+        return remote(picked.at[1], halo.at[c], far_send.at[0], halo_recv.at[c], (s + 1, core))
+
+    def far_gate(q):
         return remote(
-            side_out.at[d], side_in, side_send.at[d], side_recv.at[0], (s - 1 + 2 * d, target)
+            picked.at[1], gated.at[q], far_send.at[1], gate_recv.at[q], (s + 1, 6 + core)
+        )
+
+    def side_copy(d, target, k=0):
+        return remote(
+            side_out.at[d],
+            side_in,
+            side_send.at[2 * k + d],
+            side_recv.at[0],
+            (s - 1 + 2 * d, target),
         )
 
     def there_of(j):
@@ -276,14 +294,33 @@
         return remote(own.at[c], own.at[c], own_send.at[j], own_recv.at[c], (s, target))
 
     def when_list(d, act):
-        @pl.when(distant[d])
-        def _():
+        if d == 1:
+
+            @pl.when(distant[1] & (front == 0))
+            def _():
+                act(far_up())
+
+            @pl.when(distant[1] & (chip == 3))
+            def _():
+                act(side_copy(1, core, 0))
+                act(side_copy(1, 2 + core, 1))
+
             for q in range(2):
-                act(far_copy(d, q))
-
-            @pl.when(front == 0)
+
+                @pl.when(distant[1] & (chip == q))
+                def _():
+                    act(far_gate(q))
+
+        else:
+
+            @pl.when(distant[0])
             def _():
-                act(side_copy(d, flip))
+                for q in range(2):
+                    act(far_down(q))
+
+            @pl.when(distant[0] & (front == 0))
+            def _():
+                act(side_copy(0, flip))
 
         @pl.when(near[d] & (upper != d))
         def _():
@@ -399,6 +436,33 @@
         landed(own, own_recv, i).wait_recv()
         forward(own, own_fwd, own_recv, i, j - 1).start()
 
+    def gate_copy(q, k):
+        i = 2 * q + core
+        return remote(
+            gated.at[q], halo.at[i], gate_send.at[2 * q + k], halo_recv.at[i], (s, 2 * k + core)
+        )
+
+    def gate_pass(q):
+        i = 2 * q + core
+        return remote(
+            halo.at[i], halo.at[i], gate_send.at[q - 2], halo_recv.at[i], (s, 2 + core)
+        )
+
+    @pl.when(distant[0] & (chip == 3))
+    def _():
+        for q in range(2):
+            remote(gated.at[q], gated.at[q], gate_recv.at[q], gate_recv.at[q], (s, sib)).wait_recv()
+            for k in range(2):
+                gate_copy(q, k).start()
+
+    @pl.when(distant[0] & (chip == 0))
+    def _():
+        for q in (3, 2):
+            i = 2 * q + core
+            landed(halo, halo_recv, i).wait_recv()
+            gate_pass(q).start()
+            forward(halo, halo_fwd, halo_recv, i, q).start()
+
     @pl.when(plane_near)
     def _():
         for q in range(1, 4):
@@ -420,10 +484,13 @@
 
     @pl.when(plane_far)
     def _():
-        for q in range(4):
-            i = 2 * (3 - q) + core
-            landed(halo, halo_recv, i).wait_recv()
-            forward(halo, halo_fwd, halo_recv, i, q).start()
+        for q in (3, 2, 1, 0):
+            i = 2 * q + core
+
+            @pl.when((s < slabs // 2) | (chip == 1) | (q < 2))
+            def _():
+                landed(halo, halo_recv, i).wait_recv()
+                forward(halo, halo_fwd, halo_recv, i, q).start()
 
     @pl.when(has_halo)
     def _():
@@ -499,6 +566,17 @@
 
     for d in range(2):
         when_pass(d, lambda copy: copy.wait_send())
+
+    @pl.when(distant[0] & (chip == 3))
+    def _():
+        for q in range(2):
+            for k in range(2):
+                gate_copy(q, k).wait_send()
+
+    @pl.when(distant[0] & (chip == 0))
+    def _():
+        for q in (3, 2):
+            gate_pass(q).wait_send()
 
     @pl.when(has_halo)
     def _():
@@ -568,6 +646,7 @@
             pltpu.VMEM((8, ROWS, send * 3 // 4), BF16),
             pltpu.VMEM((2, ROWS, send * 3 // 4), BF16),
             pltpu.VMEM((ROWS, send * 3 // 4), BF16),
+            pltpu.VMEM((2, ROWS, send * 3 // 4), BF16),
             pltpu.VMEM((2, ROWS, send // 4), BF16),
             pltpu.VMEM((ROWS, send // 4), BF16),
             pltpu.VMEM((9 * ROWS, points + send), BF16),
@@ -593,6 +672,8 @@
             dma((1,)),
             dma((3,)),
             dma((2,)),
+            dma((4,)),
+            dma((4,)),
             dma((1,)),
             dma((7,)),
             dma((8,)),

time: 25.5 us -> 25 us (0.980)
  the two profiles are of different devices: /device:TPU:31 before, /device:TPU:225 now
where the time goes in v5:
time: 25 us; the launch traced here: 24.9 us
  Pallas kernels  23.5 us (94%)
  local copies, waits for them, and re-layouts  1.3 us (5%)
    pallas_call x1, Pallas kernels, shards(): pl.pallas_call(functools.partial(kernel, slabs), out_shape=jax.ShapeDtype...  23.5 us
    unnamed x1, local copies, waits for them, and re-layouts  1.3 us

profile of v5, /device:TPU:225, one launch (start us, length us, event | category | flops | bytes accessed | tf_op | source)
XLA Modules:
  0.0 24.9 jit_solution(11775050974182210244)
XLA Ops:
  0.0 23.5 %shard_map.127 = f32[12,128]{1,0:T(8,128)} custom-call(bf16[12,2048]{1,0:T(8,128)(2,1)} %feat_h.1, bf16[3,2048]{1,0:T(4,128)(2,1)} %coords_h.1, s32[2,1024]{1,0:T(2,128)} %send_rows_h.1, s32[2]{0:T(128)} %bitcast.8, s32[128,128]{1,0:T(8,128)} %nbr_h.1, s32[128]{0:T(128)} %counts_h.1, bf16[6,80]{1,0:T(8,128)(2,1)} %bitcast.7, bf16[80,96]{1,0:T(8,128)(2,1)} %feat_weight_h.1, ...), custom_call_target="tpu_custom_call" | custom-call | tf_op jit(solution)/shard_map/pallas_call | solution.py:638
  23.6 1.3 %copy.15 = f32[12,128]{1,0:T(8,128)} copy(f32[12,128]{1,0:T(8,128)} %shard_map.127) | data formatting | bytes 12288

commit v6 on v4

--- a/solution.py
+++ b/solution.py
@@ -102,9 +102,16 @@
     core = c % 2
     sib = c + 1 - 2 * core
     front = 1 - chip // 2
+    ends = 1 - (chip + 1) // 2 % 2
     half = s * 2 // slabs
-    upper = jnp.where(half == 0, front, 1 - front)
-    rank = 2 * (chip % 2) + core
+    begins = s == slabs // 2
+
+    def works_upper(slab):
+        usual = jnp.where(slab * 2 // slabs == 0, front, 1 - front)
+        return jnp.where(slab == slabs // 2, ends, usual)
+
+    upper = works_upper(s)
+    rank = 2 * jnp.where(begins, jnp.where(ends == 1, chip // 3, chip - 1), chip % 2) + core
     place = 4 * upper + rank
     early = (half == 0) & (front == 1)
     has_up = s < slabs - 1
@@ -115,8 +122,7 @@
     near = tuple(has[d] & jnp.logical_not(distant[d]) for d in range(2))
     plane_far = jnp.where(upper == 1, s == slabs // 2 - 1, s == slabs // 2)
     plane_near = has_halo & jnp.logical_not(plane_far)
-    flip = 2 * (3 - chip) + core
-    beside = 2 * (chip + 1 - 2 * (chip % 2)) + core
+    beside = 2 * jnp.where(begins, 3 - chip, chip + 1 - 2 * (chip % 2)) + core
 
     points = feat.shape[1]
     send = send_rows.shape[1]
@@ -138,7 +144,7 @@
                 barrier, inc=1, device_id=(s - 1 + 2 * d, c), device_id_type=MESH
             )
 
-        @pl.when(distant[d] & (front == 1))
+        @pl.when(distant[d] & (upper == d))
         def _():
             for q in range(4):
                 pl.semaphore_signal(
@@ -258,7 +264,7 @@
             halo.at[c],
             far_send.at[q],
             halo_recv.at[c],
-            (s - 1 + 2 * d, 2 * q + core),
+            (s - 1 + 2 * d, 2 * (q + d) + core),
         )
 
     def side_copy(d, target):
@@ -281,16 +287,19 @@
             for q in range(2):
                 act(far_copy(d, q))
 
-            @pl.when(front == 0)
+            @pl.when((ends if d == 1 else 1 - front) == 1)
             def _():
-                act(side_copy(d, flip))
-
-        @pl.when(near[d] & (upper != d))
+                there = jnp.where(chip == 3, 1, 2) if d == 1 else 3 - chip
+                act(side_copy(d, 2 * there + core))
+
+        used = works_upper(s - 1 + 2 * d) == 1 - d
+
+        @pl.when(near[d] & used)
         def _():
             act(list_copy(d, True))
             act(side_copy(d, c))
 
-        @pl.when(near[d] & (upper == d))
+        @pl.when(near[d] & jnp.logical_not(used))
         def _():
             act(list_copy(d, False))
 
@@ -314,7 +323,7 @@
             halo.at[c],
             z_send.at[1 + q],
             halo_recv.at[c],
-            (s, 2 * (2 * front + q) + core),
+            (s, 2 * jnp.where(begins, jnp.where(ends == 1, 1 + q, 3 * q), 2 * front + q) + core),
         )
 
     def when_pass(d, act):

time: 25.5 us -> 24.4 us (0.957)
  Pallas kernels: 24.1 us -> 23 us
    pallas_call x1, Pallas kernels: 24.1 us -> 23 us  [shards(): pl.pallas_call(functools.partial(kernel, slabs), out_shape=jax.ShapeDtype...]
where the time goes in v6:
time: 24.4 us; the launch traced here: 24.3 us
  Pallas kernels  23 us (94%)
  local copies, waits for them, and re-layouts  1.3 us (5%)
    pallas_call x1, Pallas kernels, shards(): pl.pallas_call(functools.partial(kernel, slabs), out_shape=jax.ShapeDtype...  23 us
    unnamed x1, local copies, waits for them, and re-layouts  1.3 us

profile of v6, /device:TPU:31, one launch (start us, length us, event | category | flops | bytes accessed | tf_op | source)
XLA Modules:
  0.0 24.3 jit_solution(4451529229228499437)
XLA Ops:
  0.0 23.0 %shard_map.127 = f32[12,128]{1,0:T(8,128)} custom-call(bf16[12,2048]{1,0:T(8,128)(2,1)} %feat_h.1, bf16[3,2048]{1,0:T(4,128)(2,1)} %coords_h.1, s32[2,1024]{1,0:T(2,128)} %send_rows_h.1, s32[2]{0:T(128)} %bitcast.8, s32[128,128]{1,0:T(8,128)} %nbr_h.1, s32[128]{0:T(128)} %counts_h.1, bf16[6,80]{1,0:T(8,128)(2,1)} %bitcast.7, bf16[80,96]{1,0:T(8,128)(2,1)} %feat_weight_h.1, ...), custom_call_target="tpu_custom_call" | custom-call | tf_op jit(solution)/shard_map/pallas_call | solution.py:569
  23.0 1.3 %copy.15 = f32[12,128]{1,0:T(8,128)} copy(f32[12,128]{1,0:T(8,128)} %shard_map.127) | data formatting | bytes 12288

commit v7 on v6

--- a/solution.py
+++ b/solution.py
@@ -339,17 +339,19 @@
     def pass_near():
         for d in range(2):
 
+            @pl.when(near[d] & (upper != d))
+            def _():
+                remote(passing, passing, pass_recv.at[0], pass_recv.at[0], (s, sib)).wait_recv()
+                for q in range(2):
+                    other_plane(q).start()
+
+        for d in range(2):
+
             @pl.when(near[d] & (upper == d))
             def _():
                 landed(halo, halo_recv, c).wait_recv()
                 same_plane().start()
                 forward(halo, halo_fwd, halo_recv, c, 0).start()
-
-            @pl.when(near[d] & (upper != d))
-            def _():
-                remote(passing, passing, pass_recv.at[0], pass_recv.at[0], (s, sib)).wait_recv()
-                for q in range(2):
-                    other_plane(q).start()
 
     for load in loads[6:]:
         load.wait()
@@ -408,13 +410,6 @@
         landed(own, own_recv, i).wait_recv()
         forward(own, own_fwd, own_recv, i, j - 1).start()
 
-    @pl.when(plane_near)
-    def _():
-        for q in range(1, 4):
-            i = 2 * ((chip + q) % 4) + core
-            landed(halo, halo_recv, i).wait_recv()
-            forward(halo, halo_fwd, halo_recv, i, q).start()
-
     for j in range(4):
         landed(own, own_recv, 2 * ((chip + j) % 4) + 1 - core).wait_recv()
 
@@ -425,7 +420,23 @@
             [rest[:, g * tail : (g + 1) * tail] for g in range(3)] + [jnp.zeros((4, tail), F32)], axis=0
         )
         table[i * ROWS : (i + 1) * ROWS, body:points] = rest.astype(BF16)
-    grid[...] = jnp.dot(table[:, 0:points], hot[0:points, :], preferred_element_type=F32)
+    cut = pairs * 4 // 8
+
+    def gather_own(low, high):
+        grid[:, low:high] = jnp.dot(
+            table[:, 0:points], hot[0:points, low:high], preferred_element_type=F32
+        )
+
+    gather_own(0, cut)
+
+    @pl.when(plane_near)
+    def _():
+        for q in range(1, 4):
+            i = 2 * ((chip + q) % 4) + core
+            landed(halo, halo_recv, i).wait_recv()
+            forward(halo, halo_fwd, halo_recv, i, q).start()
+
+    gather_own(cut, pairs)
 
     @pl.when(plane_far)
     def _():

time: 24.4 us -> 24 us (0.984)
  Pallas kernels: 23 us -> 22.6 us
    pallas_call x1, Pallas kernels: 23 us -> 22.6 us  [shards(): pl.pallas_call(functools.partial(kernel, slabs), out_shape=jax.ShapeDtype...]
where the time goes in v7:
time: 24 us; the launch traced here: 23.9 us
  Pallas kernels  22.6 us (94%)
  local copies, waits for them, and re-layouts  1.3 us (5%)
    pallas_call x1, Pallas kernels, shards(): pl.pallas_call(functools.partial(kernel, slabs), out_shape=jax.ShapeDtype...  22.6 us
    unnamed x1, local copies, waits for them, and re-layouts  1.3 us

profile of v7, /device:TPU:31, one launch (start us, length us, event | category | flops | bytes accessed | tf_op | source)
XLA Modules:
  0.0 23.9 jit_solution(18244230960267810586)
XLA Ops:
  0.0 22.6 %shard_map.127 = f32[12,128]{1,0:T(8,128)} custom-call(bf16[12,2048]{1,0:T(8,128)(2,1)} %feat_h.1, bf16[3,2048]{1,0:T(4,128)(2,1)} %coords_h.1, s32[2,1024]{1,0:T(2,128)} %send_rows_h.1, s32[2]{0:T(128)} %bitcast.8, s32[128,128]{1,0:T(8,128)} %nbr_h.1, s32[128]{0:T(128)} %counts_h.1, bf16[6,80]{1,0:T(8,128)(2,1)} %bitcast.7, bf16[80,96]{1,0:T(8,128)(2,1)} %feat_weight_h.1, ...), custom_call_target="tpu_custom_call" | custom-call | tf_op jit(solution)/shard_map/pallas_call | solution.py:580
  22.6 1.3 %copy.15 = f32[12,128]{1,0:T(8,128)} copy(f32[12,128]{1,0:T(8,128)} %shard_map.127) | data formatting | bytes 12288

commit v8 on v7

--- a/solution.py
+++ b/solution.py
@@ -580,7 +580,7 @@
     return pl.pallas_call(
         functools.partial(kernel, slabs),
         out_shape=jax.ShapeDtypeStruct((12, 128), F32),
-        in_specs=[pl.BlockSpec(memory_space=pl.ANY)] * len(args),
+        in_specs=[pl.BlockSpec(memory_space=pltpu.HBM)] * len(args),
         out_specs=pl.BlockSpec(memory_space=pltpu.VMEM),
         scratch_shapes=held
         + [
@@ -618,9 +618,9 @@
             dma((8,)),
         ],
         compiler_params=pltpu.CompilerParams(
-            collective_id=0, has_side_effects=True, vmem_limit_bytes=60 * 2**20
+            collective_id=0, has_side_effects=True, vmem_limit_bytes=48 * 2**20
         ),
-    )(*args)
+    )(*[pltpu.with_memory_space_constraint(a, pltpu.HBM) for a in args])
 
 
 def solution(mesh):

time: 24 us -> 22.7 us (0.946)
  local copies, waits for them, and re-layouts: 1.3 us -> 0.6 us
  Pallas kernels: 22.6 us -> 22 us
    unnamed x1, local copies, waits for them, and re-layouts: 1.3 us -> 0.6 us
    pallas_call x1, Pallas kernels: 22.6 us -> 22 us  [shards(): pl.pallas_call(functools.partial(kernel, slabs), out_shape=jax.ShapeDtype...]
where the time goes in v8:
time: 22.7 us; the launch traced here: 22.6 us
  Pallas kernels  22 us (97%)
  local copies, waits for them, and re-layouts  0.6 us (3%)
    pallas_call x1, Pallas kernels, shards(): pl.pallas_call(functools.partial(kernel, slabs), out_shape=jax.ShapeDtype...  22 us
    unnamed x1, local copies, waits for them, and re-layouts  0.6 us

profile of v8, /device:TPU:31, one launch (start us, length us, event | category | flops | bytes accessed | tf_op | source)
XLA Modules:
  0.0 22.6 jit_solution(16941095688609220797)
XLA Ops:
  0.0 22.0 %shard_map.127 = f32[12,128]{1,0:T(8,128)S(1)} custom-call(bf16[12,2048]{1,0:T(8,128)(2,1)} %feat_h.1, bf16[3,2048]{1,0:T(4,128)(2,1)} %coords_h.1, s32[2,1024]{1,0:T(2,128)} %send_rows_h.1, s32[2]{0:T(128)} %bitcast.8, s32[128,128]{1,0:T(8,128)} %nbr_h.1, s32[128]{0:T(128)} %counts_h.1, bf16[6,80]{1,0:T(8,128)(2,1)} %bitcast.7, ...), custom_call_target="tpu_custom_call" | custom-call | tf_op jit(solution)/shard_map/pallas_call | solution.py:580
  22.0 0.6 %copy.15 = f32[12,128]{1,0:T(8,128)} copy(f32[12,128]{1,0:T(8,128)S(1)} %shard_map.127) | data formatting | bytes 12288

commit v9 on v8

--- a/solution.py
+++ b/solution.py
@@ -501,7 +501,7 @@
     res[...] = acc / number[None]
 
     def res_copy(j):
-        target = (c + j) % 8
+        target = sib if j == 7 else 2 * there_of((j + 1) // 2) + (j - 1) % 2
         return remote(
             res.at[target], rcv.at[place], res_send.at[j - 1], res_recv.at[place], (s, target)
         )
@@ -537,6 +537,10 @@
         upper_rows = jnp.where(group == (i + 4) % 8, rcv[i], upper_rows)
     out[0:8, :] = lower_rows
     out[8:12, :] = pltpu.roll(upper_rows, 64, 1)[0:4, :]
+
+
+def finish(source, out):
+    out[...] = source[...]
 
 
 def shards(
@@ -577,7 +581,7 @@
     held = [
         (pltpu.SMEM if i in (3, 5) else pltpu.VMEM)(a.shape, a.dtype) for i, a in enumerate(args)
     ]
-    return pl.pallas_call(
+    result = pl.pallas_call(
         functools.partial(kernel, slabs),
         out_shape=jax.ShapeDtypeStruct((12, 128), F32),
         in_specs=[pl.BlockSpec(memory_space=pltpu.HBM)] * len(args),
@@ -621,6 +625,13 @@
             collective_id=0, has_side_effects=True, vmem_limit_bytes=48 * 2**20
         ),
     )(*[pltpu.with_memory_space_constraint(a, pltpu.HBM) for a in args])
+    return pl.pallas_call(
+        finish,
+        out_shape=jax.ShapeDtypeStruct((12, 128), F32),
+        in_specs=[pl.BlockSpec(memory_space=pltpu.VMEM)],
+        out_specs=pl.BlockSpec(memory_space=pltpu.VMEM),
+        compiler_params=pltpu.CompilerParams(vmem_limit_bytes=2**20),
+    )(result)
 
 
 def solution(mesh):

time: 22.7 us -> 22.7 us (level)
  Pallas kernels: 22 us -> 22.6 us
  local copies, waits for them, and re-layouts: 0.6 us -> 0 us
    unnamed x1 -> x0, local copies, waits for them, and re-layouts: 0.6 us -> none
    pallas_call x0 -> x1, Pallas kernels: none -> 0.6 us  [shards(): pl.pallas_call(finish, out_shape=jax.ShapeDtypeStruct((12, 128), F32), in...]
where the time goes in v9:
time: 22.7 us; the launch traced here: 22.6 us
  Pallas kernels  22.6 us (100%)
    pallas_call x1, Pallas kernels, shards(): pl.pallas_call(functools.partial(kernel, slabs), out_shape=jax.ShapeDtype...  22 us
    pallas_call x1, Pallas kernels, shards(): pl.pallas_call(finish, out_shape=jax.ShapeDtypeStruct((12, 128), F32), in...  0.6 us

profile of v9, /device:TPU:31, one launch (start us, length us, event | category | flops | bytes accessed | tf_op | source)
XLA Modules:
  0.0 22.6 jit_solution(1533964699536592721)
XLA Ops:
  0.0 22.0 %shard_map.127.source = f32[12,128]{1,0:T(8,128)S(1)} custom-call(bf16[12,2048]{1,0:T(8,128)(2,1)} %feat_h.1, bf16[3,2048]{1,0:T(4,128)(2,1)} %coords_h.1, s32[2,1024]{1,0:T(2,128)} %send_rows_h.1, s32[2]{0:T(128)} %bitcast.8, s32[128,128]{1,0:T(8,128)} %nbr_h.1, s32[128]{0:T(128)} %counts_h.1, bf16[6,80]{1,0:T(8,128)(2,1)} %bitcast.7, ...), custom_call_target="tpu_custom_call" | custom-call | tf_op jit(solution)/shard_map/pallas_call | solution.py:584
  22.0 0.6 %shard_map.128 = f32[12,128]{1,0:T(8,128)} custom-call(f32[12,128]{1,0:T(8,128)S(1)} %shard_map.127.source), custom_call_target="tpu_custom_call" | custom-call | tf_op jit(solution)/shard_map/pallas_call | solution.py:628
